TPU v7x, 32 devices: a whole 2x2x4 slice. The times are simulated.
32 devices in a mesh: layer: 4 (over z), row: 4 (over x, core), col: 2 (over y).
Axes of the slice: x: 2, y: 2, z: 4, core: 2. Of those that a mesh axis runs over, the one named last changes fastest.
Arguments:
- rhs_low: bfloat16 [4, 2, 2, 384, 512], P('layer', None, 'col'), may hold values from -6 to 6
- inv_low: bfloat16 [4, 2, 2, 384, 384], P('layer', None, 'col'), as said below
- blocks: bfloat16 [4, 4, 2, 2, 4, 384, 384], P('layer', 'row', 'col'), may hold values from -0.02734375 to 0.02734375
- targets: int32 [4, 4, 2, 2, 4], P('layer', 'row', 'col'), may hold values from 1 to 5, as said below
- rhs_anc: bfloat16 [16, 384, 512], P('row', None, ('layer', 'col')), may hold values from -6 to 6
- inv_anc: bfloat16 [16, 384, 384], P('row'), as said below
Outputs:
- solution_low: bfloat16 [4, 2, 2, 384, 512], P('layer', None, 'col', None, 'row')
- solution_anc: float32 [16, 384, 512], P('row', None, ('layer', 'col'))
Inputs may be any that keep to these rules, and one draw needn't show every extreme that they name: For each g, r, c, l the 4 values targets[g, r, c, l, :] are distinct. A value t < 2 is greater than l; a value t >= 2 names ancestor r * 4 + t - 2. `inv_low`: each block is lower triangular. `inv_anc`: each block is lower triangular.
All inputs are finite; a program needn't handle non-finite values.
Results may differ from a plain program's by a relative error of at most 0.011.
Values may be sent and summed in bfloat16 or wider, within the bound.
A program may use at most 64 MiB of HBM per device.

v0:
```python
import functools

import jax
import jax.numpy as jnp
from jax import lax
from jax.experimental import pallas as pl
from jax.experimental.pallas import tpu as pltpu
from jax.sharding import PartitionSpec as P

MESH = pl.DeviceIdType.MESH
F32 = jnp.float32
BF16 = jnp.bfloat16


def dot_t(left, right):
    return lax.dot_general(left, right, (((1,), (1,)), ((), ())), preferred_element_type=F32)


def kernel(
    sizes,
    targets_hbm,
    rhs_hbm,
    inv_hbm,
    blocks_hbm,
    rhs_anc_hbm,
    inv_anc_hbm,
    low_out,
    anc_out,
    rhs,
    inv,
    blocks0,
    blocks1,
    rhs_anc,
    inv_anc,
    x0,
    x1,
    part,
    part_in,
    right,
    base,
    packed,
    y_in,
    z_out,
    z_in,
    targets,
    load_sem,
    p_send,
    p_recv,
    x_send,
    x_recv,
    y_send,
    y_recv,
    z_send,
    z_recv,
):
    layers, rows, cols = sizes
    layer, row, col = (lax.axis_index(a) for a in ("layer", "row", "col"))
    slots = blocks0.shape[0]
    anc_row, narrow, width = rhs_anc.shape
    share = x1.shape[1]
    halves = packed.shape[2]
    per_half = anc_row // halves

    def ordered(k):
        return (row // 2 * 2 + k // 2 * 2) % rows + (row + k) % 2

    def flag(condition):
        return condition.astype(jnp.int32)

    last = layers - 1
    relayed = flag(layer == 1) * last - flag(layer != 1)
    relayed = relayed + flag(layer == last - 1) * (0 - relayed)
    opening = row + flag(row == layer) * (ordered(1) - row)
    keys = []
    for j in range(rows):
        place = 0
        for k in range(rows):
            place = place + k * flag(ordered(k) == j)
        key = place - 16 * jnp.abs(layer - j)
        key = key + 500 * flag(relayed == j) + 5000 * flag(layer == j) - 2000 * flag(opening == j)
        keys.append(key)
    order = [0] * rows
    for j in range(rows):
        rank = 0
        for other in range(rows):
            if other != j:
                rank = rank + flag(keys[other] < keys[j])
        order = [order[k] + j * flag(rank == k) for k in range(rows)]
    swap = flag(relayed == opening) * (order[1] - order[0])
    merge_order = [order[0] + swap, order[1] - swap] + order[2:]

    barrier = pltpu.get_barrier_semaphore()
    for dr in range(rows):
        for dc in range(cols):
            if dr or dc:
                pl.semaphore_signal(
                    barrier,
                    inc=1,
                    device_id={"row": (row + dr) % rows, "col": (col + dc) % cols},
                    device_id_type=MESH,
                )
    for dl in range(1, layers):
        pl.semaphore_signal(
            barrier, inc=1, device_id={"layer": (layer + dl) % layers}, device_id_type=MESH
        )

    loads = [
        pltpu.make_async_copy(inv_hbm.at[0], inv.at[0], load_sem.at[0]),
        pltpu.make_async_copy(rhs_hbm.at[0], rhs.at[0], load_sem.at[1]),
        pltpu.make_async_copy(blocks_hbm.at[0], blocks0, load_sem.at[2]),
        pltpu.make_async_copy(inv_hbm.at[1], inv.at[1], load_sem.at[3]),
        pltpu.make_async_copy(rhs_hbm.at[1], rhs.at[1], load_sem.at[4]),
        pltpu.make_async_copy(blocks_hbm.at[1], blocks1, load_sem.at[5]),
        pltpu.make_async_copy(inv_anc_hbm, inv_anc, load_sem.at[6]),
        pltpu.make_async_copy(rhs_anc_hbm, rhs_anc, load_sem.at[7]),
        pltpu.make_async_copy(targets_hbm, targets, load_sem.at[8]),
    ]
    for load in loads:
        load.start()

    def listed(level, target):
        index, found = jnp.int32(0), jnp.int32(0)
        for s in range(slots):
            hit = (targets[level, s] == target).astype(jnp.int32)
            index = index + hit * s
            found = found + hit
        return (blocks0, blocks1)[level][index], found.astype(F32)

    def span(j):
        return pl.ds(pl.multiple_of(j * share, share), share)

    loads[0].wait()
    loads[1].wait()
    first = jnp.dot(inv[0], rhs[0], preferred_element_type=F32)
    x0[...] = first.T.astype(BF16)

    loads[8].wait()
    loads[2].wait()
    goal = (row + rows - 1) % rows
    active = goal < cols
    owner = (1 + col) % rows

    def p_copy(k):
        j = ordered(k)
        return pltpu.make_async_remote_copy(
            src_ref=part.at[j],
            dst_ref=part_in.at[col],
            send_sem=p_send.at[k],
            recv_sem=p_recv.at[col],
            device_id={"row": j, "col": goal},
            device_id_type=MESH,
        )

    pl.semaphore_wait(barrier, rows * cols - 1 + layers - 1)

    @pl.when(active)
    def _():
        block, found = listed(0, 1)
        for k in range(rows):
            j = ordered(k)
            value = dot_t(x0[span(j), :], block) * found
            part[j] = value.astype(BF16)
            if k == 0:

                @pl.when(goal != col)
                def _():
                    p_copy(0).start()

                @pl.when(goal == col)
                def _():
                    part_in[col] = part[row]

            else:
                p_copy(k).start()

    for j in range(rows):

        @pl.when(row == j)
        def _():
            low_out[0] = x0[j * share : (j + 1) * share, :].astype(F32).T.astype(BF16)

    for a in range(anc_row):
        block, found = listed(0, a + 2)
        base[:, a * width : (a + 1) * width] = dot_t(x0[...], block) * found

    loads[3].wait()
    loads[4].wait()
    for j in range(rows):

        @pl.when(row == j)
        def _():
            right[...] = rhs[1, :, j * share : (j + 1) * share].astype(F32).T

    for cc in range(cols):

        @pl.when(jnp.logical_or(col != cc, row != owner))
        def _():
            pltpu.make_async_remote_copy(
                src_ref=part.at[0],
                dst_ref=part_in.at[cc],
                send_sem=p_send.at[0],
                recv_sem=p_recv.at[cc],
                device_id={"row": row, "col": col},
                device_id_type=MESH,
            ).wait_recv()

    total = part_in[0].astype(F32)
    for cc in range(1, cols):
        total = total + part_in[cc].astype(F32)
    residual = (right[...] - total).astype(BF16)
    x1[row] = dot_t(residual, inv[1]).astype(BF16)

    def x_copy(k, slot):
        return pltpu.make_async_remote_copy(
            src_ref=x1.at[slot],
            dst_ref=x1.at[slot],
            send_sem=x_send.at[k],
            recv_sem=x_recv.at[slot],
            device_id={"row": ordered(k)},
            device_id_type=MESH,
        )

    for k in range(1, rows):
        x_copy(k, row).start()

    def y_copy(d, j, h):
        cc = (col + d) % cols
        return pltpu.make_async_remote_copy(
            src_ref=packed.at[cc, j, h],
            dst_ref=y_in.at[d - 1, j, h],
            send_sem=y_send.at[d - 1, j, h],
            recv_sem=y_recv.at[d - 1, j, h],
            device_id={"col": cc},
            device_id_type=MESH,
        )

    loads[5].wait()
    for k in range(rows):
        j = order[k]

        @pl.when(j != row)
        def _():
            x_copy(1, j).wait_recv()

        for a in range(anc_row):
            block, found = listed(1, a + 2)
            at = slice(a * width, (a + 1) * width)
            value = base[span(j), at] + dot_t(x1[j], block) * found
            value = value.astype(BF16)
            for cc in range(cols):
                within = a % per_half * width
                packed[cc, j, a // per_half, :, within : within + width] = value[
                    cc * narrow : (cc + 1) * narrow
                ]
            if a % per_half == per_half - 1:
                for d in range(1, cols):
                    y_copy(d, j, a // per_half).start()
        if k == 0:
            low_out[1] = x1[row].astype(F32).T.astype(BF16)

    def z_copy(j, slot, target, h):
        return pltpu.make_async_remote_copy(
            src_ref=z_out.at[j, h],
            dst_ref=z_in.at[slot, h],
            send_sem=z_send.at[j, h],
            recv_sem=z_recv.at[slot, h],
            device_id={"layer": target},
            device_id_type=MESH,
        )

    def merge(j, h):
        for d in range(1, cols):
            y_copy(d, j, h).wait_recv()
        merged = packed[col, j, h].astype(F32)
        for d in range(1, cols):
            merged = merged + y_in[d - 1, j, h].astype(F32)

        @pl.when(jnp.logical_and(j == last, layer == 1))
        def _():
            z_copy(j, layers, layer, h).wait_recv()
            z_out[j, h] = (merged + z_in[layers, h].astype(F32)).astype(BF16)
            z_copy(j, layer, j, h).start()

        @pl.when(jnp.logical_and(j == 0, layer == last - 1))
        def _():
            z_copy(j, layers + 1, layer, h).wait_recv()
            z_out[j, h] = (merged + z_in[layers + 1, h].astype(F32)).astype(BF16)
            z_copy(j, layer, j, h).start()

        @pl.when(jnp.logical_and(j == last, layer == 0))
        def _():
            z_out[j, h] = merged.astype(BF16)
            z_copy(j, layers, 1, h).start()

        @pl.when(jnp.logical_and(j == 0, layer == last))
        def _():
            z_out[j, h] = merged.astype(BF16)
            z_copy(j, layers + 1, last - 1, h).start()

        direct = jnp.logical_and(j != layer, j != relayed)
        direct = jnp.logical_and(direct, jnp.abs(layer - j) != last)

        @pl.when(direct)
        def _():
            z_out[j, h] = merged.astype(BF16)
            z_copy(j, layer, j, h).start()

        @pl.when(j == layer)
        def _():
            z_in[layer, h] = merged.astype(BF16)

    for j in merge_order:
        for h in range(halves):
            merge(j, h)

    loads[6].wait()
    loads[7].wait()
    for s in range(layers):

        @pl.when(jnp.abs(layer - s) == last)
        def _():
            z_in[s] = jnp.zeros_like(z_in[s])

        @pl.when(jnp.logical_and(layer != s, jnp.abs(layer - s) != last))
        def _():
            for h in range(halves):
                z_copy(s, s, layer, h).wait_recv()

    for a in range(anc_row):
        residual = rhs_anc[a].astype(F32)
        for s in range(layers):
            within = a % per_half * width
            piece = z_in[s, a // per_half, :, within : within + width]
            residual = residual - piece.astype(F32)
        anc_out[a] = dot_t(residual.astype(BF16), inv_anc[a])


    @pl.when(active)
    def _():
        for k in range(rows):
            if k == 0:

                @pl.when(goal != col)
                def _():
                    p_copy(0).wait_send()

            else:
                p_copy(k).wait_send()

    for k in range(1, rows):
        x_copy(k, row).wait_send()
    for k in range(rows):
        j = ordered(k)
        for d in range(1, cols):
            for h in range(halves):
                y_copy(d, j, h).wait_send()

        @pl.when(j != layer)
        def _():
            for h in range(halves):
                z_copy(j, layer, j, h).wait_send()


def hand_over(low, anc, low_out, anc_out, sem):
    first = pltpu.make_async_copy(anc, anc_out, sem.at[0])
    second = pltpu.make_async_copy(low, low_out, sem.at[1])
    first.start()
    second.start()
    first.wait()
    second.wait()


def on_device(sizes, rhs_low, inv_low, blocks, targets, rhs_anc, inv_anc):
    layers, rows, cols = sizes
    levels, slots = blocks.shape[3], blocks.shape[4]
    width, cases = rhs_low.shape[3], rhs_low.shape[4]
    anc_row, narrow = rhs_anc.shape[0], rhs_anc.shape[2]
    share = cases // rows
    halves = 2 if anc_row % 2 == 0 else 1
    assert levels == 2 and layers == rows and layers > 3 and cols <= rows and cols * narrow == share
    any_space = pl.BlockSpec(memory_space=pltpu.HBM)
    dma = pltpu.SemaphoreType.DMA
    low, anc = pl.pallas_call(
        functools.partial(kernel, sizes),
        out_shape=(
            pltpu.VMEM((levels, width, share), BF16),
            pltpu.VMEM((anc_row, narrow, width), F32),
        ),
        in_specs=[any_space] * 6,
        out_specs=(pl.BlockSpec(memory_space=pltpu.VMEM), pl.BlockSpec(memory_space=pltpu.VMEM)),
        scratch_shapes=[
            pltpu.VMEM((levels, width, cases), BF16),
            pltpu.VMEM((levels, width, width), BF16),
            pltpu.VMEM((slots, width, width), BF16),
            pltpu.VMEM((slots, width, width), BF16),
            pltpu.VMEM((anc_row, narrow, width), BF16),
            pltpu.VMEM((anc_row, width, width), BF16),
            pltpu.VMEM((cases, width), BF16),
            pltpu.VMEM((rows, share, width), BF16),
            pltpu.VMEM((rows, share, width), BF16),
            pltpu.VMEM((cols, share, width), BF16),
            pltpu.VMEM((share, width), F32),
            pltpu.VMEM((cases, anc_row * width), F32),
            pltpu.VMEM((cols, rows, halves, narrow, anc_row * width // halves), BF16),
            pltpu.VMEM((cols - 1, rows, halves, narrow, anc_row * width // halves), BF16),
            pltpu.VMEM((layers, halves, narrow, anc_row * width // halves), BF16),
            pltpu.VMEM((layers + 2, halves, narrow, anc_row * width // halves), BF16),
            pltpu.SMEM((levels, slots), jnp.int32),
            dma((9,)),
            dma((rows,)),
            dma((cols,)),
            dma((rows,)),
            dma((rows,)),
            dma((cols - 1, rows, halves)),
            dma((cols - 1, rows, halves)),
            dma((layers, halves)),
            dma((layers + 2, halves)),
        ],
        compiler_params=pltpu.CompilerParams(
            collective_id=0, has_side_effects=True, vmem_limit_bytes=56 * 1024 * 1024
        ),
    )(
        targets.reshape(levels, slots),
        rhs_low.reshape(levels, width, cases),
        inv_low.reshape(levels, width, width),
        blocks.reshape(levels, slots, width, width),
        rhs_anc.transpose(0, 2, 1),
        inv_anc,
    )
    low, anc = pl.pallas_call(
        hand_over,
        out_shape=(
            jax.ShapeDtypeStruct(low.shape, low.dtype),
            jax.ShapeDtypeStruct(anc.shape, anc.dtype),
        ),
        in_specs=[pl.BlockSpec(memory_space=pltpu.VMEM)] * 2,
        out_specs=(any_space, any_space),
        scratch_shapes=[dma((2,))],
        compiler_params=pltpu.CompilerParams(vmem_limit_bytes=4 * 1024 * 1024),
    )(low, anc)
    return low[None, :, None], anc.transpose(0, 2, 1)


def solution(mesh):
    sizes = tuple(mesh.shape[a] for a in ("layer", "row", "col"))
    in_specs = (
        P("layer", None, "col", None, None),
        P("layer", None, "col", None, None),
        P("layer", "row", "col", None, None, None, None),
        P("layer", "row", "col", None, None),
        P("row", None, ("layer", "col")),
        P("row", None, None),
    )
    out_specs = (P("layer", None, "col", None, "row"), P("row", None, ("layer", "col")))
    return jax.shard_map(
        functools.partial(on_device, sizes),
        mesh=mesh,
        in_specs=in_specs,
        out_specs=out_specs,
        check_vma=False,
    )
```

profile of v0, /device:TPU:6, one launch (start us, length us, event | category | flops | bytes accessed | tf_op | source)
XLA Modules:
  0.0 38.4 jit_solution(12424388328412082383)
XLA Ops:
  0.6 36.9 %shard_map.77 = (bf16[2,384,128]{2,1,0:T(8,128)(2,1)S(1)}, f32[4,64,384]{2,1,0:T(8,128)S(1)}) custom-call(s32[2,4]{1,0:T(2,128)} %bitcast.13, bf16[2,384,512]{2,1,0:T(8,128)(2,1)} %bitcast.10, bf16[2,384,384]{2,1,0:T(8,128)(2,1)} %bitcast.11, bf16[2,4,384,384]{3,2,1,0:T(8,128)(2,1)} %bitcast.9, bf16[4,64,384]{2,1,0:T(8,128)(2,1)} %bitcast.12, ...), custom_call_target="tpu_custom_call" | custom-call | tf_op jit(solution)/shard_map/pallas_call | solution.py:383
  37.5 0.8 %shard_map.78 = (bf16[2,384,128]{2,1,0:T(8,128)(2,1)}, f32[4,64,384]{2,1,0:T(8,128)}) custom-call(bf16[2,384,128]{2,1,0:T(8,128)(2,1)S(1)} %get-tuple-element.6.low, f32[4,64,384]{2,1,0:T(8,128)S(1)} %get-tuple-element.7.anc), custom_call_target="tpu_custom_call" | custom-call | tf_op jit(solution)/shard_map/pallas_call | solution.py:430
where the time goes:
time: 38.5 us; the launch traced here: 38.4 us
  Pallas kernels  37.7 us (98%)
  between operations  0.64 us (2%)
    pallas_call x1, Pallas kernels, on_device(): pl.pallas_call(functools.partial(kernel, sizes), out_shape=(pltpu.VMEM((l...  36.9 us
    pallas_call x1, Pallas kernels, on_device(): pl.pallas_call(hand_over, out_shape=(jax.ShapeDtypeStruct(low.shape, low....  0.83 us

commit v1 on v0

v1 whole, which is shorter than its diff:
```python
import contextlib
import functools

import jax
import jax.numpy as jnp
from jax import lax
from jax.experimental import pallas as pl
from jax.experimental.pallas import tpu as pltpu
from jax.sharding import PartitionSpec as P

MESH = pl.DeviceIdType.MESH
F32 = jnp.float32
BF16 = jnp.bfloat16


def scope(name):
    return contextlib.nullcontext()


def dot_t(left, right):
    return lax.dot_general(left, right, (((1,), (1,)), ((), ())), preferred_element_type=F32)


def flag(condition):
    return condition.astype(jnp.int32)


def ranked(layer, layers):
    keys = []
    for j in range(layers):
        keys.append(flag(layer == j) * 1000 * layers - 2 * layers * jnp.abs(layer - j) - j)
    order = [0] * layers
    for j in range(layers):
        rank = 0
        for other in range(layers):
            if other != j:
                rank = rank + flag(keys[other] < keys[j])
        order = [order[k] + j * flag(rank == k) for k in range(layers)]
    return order


def kernel(
    sizes,
    targets_hbm,
    rhs_hbm,
    inv_hbm,
    blocks_hbm,
    rhs_anc_hbm,
    inv_anc_hbm,
    low_out,
    anc_out,
    rhs,
    inv,
    blocks0,
    blocks1,
    rhs_anc,
    inv_anc,
    x0,
    x1,
    part,
    part_in,
    rhs_t,
    base,
    packed,
    y_in,
    z_out,
    z_in,
    targets,
    load_sem,
    p_send,
    p_recv,
    x_send,
    x_recv,
    y_send,
    y_recv,
    z_send,
    z_recv,
):
    layers, rows, cols = sizes
    layer, row, col = (lax.axis_index(a) for a in ("layer", "row", "col"))
    slots = blocks0.shape[0]
    anc_row, narrow, width = rhs_anc.shape
    share = x1.shape[1]
    halves = packed.shape[2]
    per_half = anc_row // halves
    chips = rows // 2
    last = layers - 1

    chip, core = row // 2, row % 2
    mate = row + 1 - 2 * core
    order = ranked(layer, layers)
    goal = (row + rows - 1) % rows
    active = goal < cols
    owner = (1 + col) % rows

    barrier = pltpu.get_barrier_semaphore()

    def greet(device):
        pl.semaphore_signal(barrier, inc=1, device_id=device, device_id_type=MESH)

    greet({"row": mate})
    for d in range(1, cols):
        greet({"col": (col + d) % cols})
    for step in (-1, 1):

        @pl.when(jnp.logical_and(layer + step >= 0, layer + step < layers))
        def _():
            greet({"layer": layer + step})

    for cc in range(cols):

        @pl.when(jnp.logical_or(row != owner, col != cc))
        def _():
            greet({"row": owner, "col": cc})

    @pl.when(active)
    def _():
        for r in range(rows):

            @pl.when(jnp.logical_or(row != r, col != goal))
            def _():
                greet({"row": r, "col": goal})

    met = 1 + (cols - 1) + flag(layer > 0) + flag(layer < last)
    met = met + cols - flag(row == owner)
    met = met + flag(active) * (rows - flag(col == goal))

    loads = [
        pltpu.make_async_copy(inv_hbm.at[0], inv.at[0], load_sem.at[0]),
        pltpu.make_async_copy(rhs_hbm.at[0], rhs.at[0], load_sem.at[1]),
        pltpu.make_async_copy(blocks_hbm.at[0], blocks0, load_sem.at[2]),
        pltpu.make_async_copy(inv_hbm.at[1], inv.at[1], load_sem.at[3]),
        pltpu.make_async_copy(rhs_hbm.at[1], rhs.at[1], load_sem.at[4]),
        pltpu.make_async_copy(blocks_hbm.at[1], blocks1, load_sem.at[5]),
        pltpu.make_async_copy(inv_anc_hbm, inv_anc, load_sem.at[6]),
        pltpu.make_async_copy(rhs_anc_hbm, rhs_anc, load_sem.at[7]),
        pltpu.make_async_copy(targets_hbm, targets, load_sem.at[8]),
    ]
    for load in loads:
        load.start()

    def listed(level, target):
        index, found = jnp.int32(0), jnp.int32(0)
        for s in range(slots):
            hit = (targets[level, s] == target).astype(jnp.int32)
            index = index + hit * s
            found = found + hit
        return (blocks0, blocks1)[level][index], found.astype(F32)

    def span(j):
        return pl.ds(pl.multiple_of(j * share, share), share)

    with scope("x0"):
        loads[0].wait()
        loads[1].wait()
        first = jnp.dot(inv[0], rhs[0], preferred_element_type=F32)
        x0[...] = first.T.astype(BF16)

    loads[8].wait()
    loads[2].wait()

    def p_copy(k, ch):
        return pltpu.make_async_remote_copy(
            src_ref=part.at[k],
            dst_ref=part_in.at[k // 2, col],
            send_sem=p_send.at[k, ch],
            recv_sem=p_recv.at[k // 2, col],
            device_id={"row": 2 * ch + k % 2, "col": goal},
            device_id_type=MESH,
        )

    def here(k, ch):
        return jnp.logical_and(goal == col, row == 2 * ch + k % 2)

    def part_of(k):
        block, found = listed(0, 1)
        part[k] = (dot_t(x0[span(order[k]), :], block) * found).astype(BF16)

    @pl.when(active)
    def _():
        part_of(0)

    with scope("barr"):
        pl.semaphore_wait(barrier, met)

    with scope("part"):

        @pl.when(active)
        def _():
            for k in range(rows):
                if k:
                    part_of(k)
                for ch in range(chips):

                    @pl.when(jnp.logical_not(here(k, ch)))
                    def _():
                        p_copy(k, ch).start()

                    @pl.when(here(k, ch))
                    def _():
                        part_in[k // 2, col] = part[k]

    loads[3].wait()
    loads[4].wait()
    rhs_t[...] = rhs[1].astype(F32).T

    with scope("base"):
        for a in range(anc_row):
            block, found = listed(0, a + 2)
            base[:, a * width : (a + 1) * width] = dot_t(x0[...], block) * found

    for j in range(rows):

        @pl.when(row == j)
        def _():
            low_out[0] = x0[j * share : (j + 1) * share, :].astype(F32).T.astype(BF16)

    @pl.when(layer == 0)
    def _():
        z_in[0] = jnp.zeros_like(z_in[0])

    @pl.when(layer == last)
    def _():
        z_in[layers] = jnp.zeros_like(z_in[layers])

    loads[5].wait()

    def own(m):
        return order[2 * m] + core * (order[2 * m + 1] - order[2 * m])

    def x_copy(m):
        return pltpu.make_async_remote_copy(
            src_ref=x1.at[own(m)],
            dst_ref=x1.at[own(m)],
            send_sem=x_send.at[m],
            recv_sem=x_recv.at[m],
            device_id={"row": mate},
            device_id_type=MESH,
        )

    def solve(m):
        for cc in range(cols):

            @pl.when(jnp.logical_or(col != cc, row != owner))
            def _():
                pltpu.make_async_remote_copy(
                    src_ref=part.at[0],
                    dst_ref=part_in.at[m, cc],
                    send_sem=p_send.at[0, 0],
                    recv_sem=p_recv.at[m, cc],
                    device_id={"row": mate},
                    device_id_type=MESH,
                ).wait_recv()

        total = part_in[m, 0].astype(F32)
        for cc in range(1, cols):
            total = total + part_in[m, cc].astype(F32)
        residual = (rhs_t[span(own(m)), :] - total).astype(BF16)
        x1[own(m)] = dot_t(residual, inv[1]).astype(BF16)
        x_copy(m).start()

    def y_copy(d, k, h):
        cc = (col + d) % cols
        return pltpu.make_async_remote_copy(
            src_ref=packed.at[cc, k, h],
            dst_ref=y_in.at[d - 1, k, h],
            send_sem=y_send.at[d - 1, k, h],
            recv_sem=y_recv.at[d - 1, k, h],
            device_id={"col": cc},
            device_id_type=MESH,
        )

    def products(k):
        @pl.when(core != k % 2)
        def _():
            x_copy(k // 2).wait_recv()

        j = order[k]
        for a in range(anc_row):
            block, found = listed(1, a + 2)
            at = slice(a * width, (a + 1) * width)
            value = base[span(j), at] + dot_t(x1[j], block) * found
            value = value.astype(BF16)
            within = a % per_half * width
            for cc in range(cols):
                packed[cc, k, a // per_half, :, within : within + width] = value[
                    cc * narrow : (cc + 1) * narrow
                ]
            if a % per_half == per_half - 1:
                for d in range(1, cols):
                    y_copy(d, k, a // per_half).start()

    def z_copy(k, h):
        j = order[k]
        toward = layer + 2 * flag(j > layer) - 1
        slot = j + flag(j == layer - 1) * (layers - j)
        return pltpu.make_async_remote_copy(
            src_ref=z_out.at[k, h],
            dst_ref=z_in.at[slot, h],
            send_sem=z_send.at[k, h],
            recv_sem=z_recv.at[slot, h],
            device_id={"layer": toward},
            device_id_type=MESH,
        )

    def z_wait(slot, h):
        pltpu.make_async_remote_copy(
            src_ref=z_out.at[0, h],
            dst_ref=z_in.at[slot, h],
            send_sem=z_send.at[0, h],
            recv_sem=z_recv.at[slot, h],
            device_id={"layer": (layer + 1) % layers},
            device_id_type=MESH,
        ).wait_recv()

    def merged(k, h):
        for d in range(1, cols):
            y_copy(d, k, h).wait_recv()
        value = packed[col, k, h].astype(F32)
        for d in range(1, cols):
            value = value + y_in[d - 1, k, h].astype(F32)
        return value

    def merge(k, h):
        with scope("y%d%d" % (k, h)):
            value = merged(k, h)
        j = order[k]
        passing = jnp.logical_or(
            jnp.logical_and(j > layer, layer > 0), jnp.logical_and(j < layer, layer < last)
        )

        with scope("z%d%d" % (k, h)):

            @pl.when(passing)
            def _():
                z_wait(j, h)
                z_out[k, h] = (value + z_in[j, h].astype(F32)).astype(BF16)

            @pl.when(jnp.logical_not(passing))
            def _():
                z_out[k, h] = value.astype(BF16)

        z_copy(k, h).start()

    for k in range(rows):
        if k % 2 == 0:
            with scope("x1_%d" % (k // 2)):
                solve(k // 2)
        with scope("p%d" % k):
            products(k)

    low_out[1] = x1[row].astype(F32).T.astype(BF16)
    for k in range(rows - 1):
        for h in range(halves):
            merge(k, h)

    loads[6].wait()
    loads[7].wait()
    with scope("zown"):

        @pl.when(layer > 0)
        def _():
            for h in range(halves):
                z_wait(layer, h)

        @pl.when(layer < last)
        def _():
            for h in range(halves):
                z_wait(layers, h)

    for h in range(halves):
        with scope("yown%d" % h):
            value = merged(rows - 1, h)
        with scope("fin%d" % h):
            value = value + z_in[layer, h].astype(F32) + z_in[layers, h].astype(F32)
            for within in range(per_half):
                a = h * per_half + within
                piece = value[:, within * width : (within + 1) * width]
                residual = (rhs_anc[a].astype(F32) - piece).astype(BF16)
                anc_out[a] = dot_t(residual, inv_anc[a])

    with scope("sent"):

        @pl.when(active)
        def _():
            for k in range(rows):
                for ch in range(chips):

                    @pl.when(jnp.logical_not(here(k, ch)))
                    def _():
                        p_copy(k, ch).wait_send()

        for m in range(chips):
            x_copy(m).wait_send()
        for k in range(rows):
            for h in range(halves):
                for d in range(1, cols):
                    y_copy(d, k, h).wait_send()
                if k < rows - 1:
                    z_copy(k, h).wait_send()


def hand_over(low, anc, low_out, anc_out, sem):
    first = pltpu.make_async_copy(anc, anc_out, sem.at[0])
    second = pltpu.make_async_copy(low, low_out, sem.at[1])
    first.start()
    second.start()
    first.wait()
    second.wait()


def on_device(sizes, rhs_low, inv_low, blocks, targets, rhs_anc, inv_anc):
    layers, rows, cols = sizes
    levels, slots = blocks.shape[3], blocks.shape[4]
    width, cases = rhs_low.shape[3], rhs_low.shape[4]
    anc_row, narrow = rhs_anc.shape[0], rhs_anc.shape[2]
    share = cases // rows
    halves = 2 if anc_row % 2 == 0 else 1
    chips = rows // 2
    assert levels == 2 and layers == rows and rows % 2 == 0 and cols <= rows
    assert cols * narrow == share
    any_space = pl.BlockSpec(memory_space=pltpu.HBM)
    dma = pltpu.SemaphoreType.DMA
    wide = anc_row * width // halves
    low, anc = pl.pallas_call(
        functools.partial(kernel, sizes),
        out_shape=(
            pltpu.VMEM((levels, width, share), BF16),
            pltpu.VMEM((anc_row, narrow, width), F32),
        ),
        in_specs=[any_space] * 6,
        out_specs=(pl.BlockSpec(memory_space=pltpu.VMEM), pl.BlockSpec(memory_space=pltpu.VMEM)),
        scratch_shapes=[
            pltpu.VMEM((levels, width, cases), BF16),
            pltpu.VMEM((levels, width, width), BF16),
            pltpu.VMEM((slots, width, width), BF16),
            pltpu.VMEM((slots, width, width), BF16),
            pltpu.VMEM((anc_row, narrow, width), BF16),
            pltpu.VMEM((anc_row, width, width), BF16),
            pltpu.VMEM((cases, width), BF16),
            pltpu.VMEM((rows, share, width), BF16),
            pltpu.VMEM((rows, share, width), BF16),
            pltpu.VMEM((chips, cols, share, width), BF16),
            pltpu.VMEM((cases, width), F32),
            pltpu.VMEM((cases, anc_row * width), F32),
            pltpu.VMEM((cols, rows, halves, narrow, wide), BF16),
            pltpu.VMEM((cols - 1, rows, halves, narrow, wide), BF16),
            pltpu.VMEM((rows - 1, halves, narrow, wide), BF16),
            pltpu.VMEM((layers + 1, halves, narrow, wide), BF16),
            pltpu.SMEM((levels, slots), jnp.int32),
            dma((9,)),
            dma((rows, chips)),
            dma((chips, cols)),
            dma((chips,)),
            dma((chips,)),
            dma((cols - 1, rows, halves)),
            dma((cols - 1, rows, halves)),
            dma((rows - 1, halves)),
            dma((layers + 1, halves)),
        ],
        compiler_params=pltpu.CompilerParams(
            collective_id=0, has_side_effects=True, vmem_limit_bytes=56 * 1024 * 1024
        ),
    )(
        targets.reshape(levels, slots),
        rhs_low.reshape(levels, width, cases),
        inv_low.reshape(levels, width, width),
        blocks.reshape(levels, slots, width, width),
        rhs_anc.transpose(0, 2, 1),
        inv_anc,
    )
    low, anc = pl.pallas_call(
        hand_over,
        out_shape=(
            jax.ShapeDtypeStruct(low.shape, low.dtype),
            jax.ShapeDtypeStruct(anc.shape, anc.dtype),
        ),
        in_specs=[pl.BlockSpec(memory_space=pltpu.VMEM)] * 2,
        out_specs=(any_space, any_space),
        scratch_shapes=[dma((2,))],
        compiler_params=pltpu.CompilerParams(vmem_limit_bytes=4 * 1024 * 1024),
    )(low, anc)
    return low[None, :, None], anc.transpose(0, 2, 1)


def solution(mesh):
    sizes = tuple(mesh.shape[a] for a in ("layer", "row", "col"))
    in_specs = (
        P("layer", None, "col", None, None),
        P("layer", None, "col", None, None),
        P("layer", "row", "col", None, None, None, None),
        P("layer", "row", "col", None, None),
        P("row", None, ("layer", "col")),
        P("row", None, None),
    )
    out_specs = (P("layer", None, "col", None, "row"), P("row", None, ("layer", "col")))
    return jax.shard_map(
        functools.partial(on_device, sizes),
        mesh=mesh,
        in_specs=in_specs,
        out_specs=out_specs,
        check_vma=False,
    )
```

time: 38.5 us -> 32.6 us (0.85)
  the two profiles are of different devices: /device:TPU:6 before, /device:TPU:0 now
where the time goes in v1:
time: 32.6 us; the launch traced here: 32.4 us
  Pallas kernels  31.8 us (98%)
  between operations  0.64 us (2%)
    pallas_call x1, Pallas kernels, on_device(): pl.pallas_call(functools.partial(kernel, sizes), out_shape=(pltpu.VMEM((l...  31 us
    pallas_call x1, Pallas kernels, on_device(): pl.pallas_call(hand_over, out_shape=(jax.ShapeDtypeStruct(low.shape, low....  0.83 us

profile of v1, /device:TPU:0, one launch (start us, length us, event | category | flops | bytes accessed | tf_op | source)
XLA Modules:
  0.0 32.4 jit_solution(5803046334342413682)
XLA Ops:
  0.6 31.0 %shard_map.77 = (bf16[2,384,128]{2,1,0:T(8,128)(2,1)S(1)}, f32[4,64,384]{2,1,0:T(8,128)S(1)}) custom-call(s32[2,4]{1,0:T(2,128)} %bitcast.13, bf16[2,384,512]{2,1,0:T(8,128)(2,1)} %bitcast.10, bf16[2,384,384]{2,1,0:T(8,128)(2,1)} %bitcast.11, bf16[2,4,384,384]{3,2,1,0:T(8,128)(2,1)} %bitcast.9, bf16[4,64,384]{2,1,0:T(8,128)(2,1)} %bitcast.12, ...), custom_call_target="tpu_custom_call" | custom-call | tf_op jit(solution)/shard_map/pallas_call | solution.py:425
  31.6 0.8 %shard_map.78 = (bf16[2,384,128]{2,1,0:T(8,128)(2,1)}, f32[4,64,384]{2,1,0:T(8,128)}) custom-call(bf16[2,384,128]{2,1,0:T(8,128)(2,1)S(1)} %get-tuple-element.6.low, f32[4,64,384]{2,1,0:T(8,128)S(1)} %get-tuple-element.7.anc), custom_call_target="tpu_custom_call" | custom-call | tf_op jit(solution)/shard_map/pallas_call | solution.py:472

commit v2 on v1

--- a/solution.py
+++ b/solution.py
@@ -26,9 +26,13 @@
 
 
 def ranked(layer, layers):
+    low = flag(layer < layers // 2)
+    far, near = low * (layers - 1), (1 - low) * (layers - 1)
     keys = []
     for j in range(layers):
-        keys.append(flag(layer == j) * 1000 * layers - 2 * layers * jnp.abs(layer - j) - j)
+        key = -2 * layers * jnp.abs(layer - j) - j
+        key = key - 1000 * layers * flag(far == j) + 1000 * layers * flag(near == j)
+        keys.append(key + 5000 * layers * flag(layer == j))
     order = [0] * layers
     for j in range(layers):
         rank = 0
@@ -65,6 +69,7 @@
     y_in,
     z_out,
     z_in,
+    r_in,
     targets,
     load_sem,
     p_send,
@@ -75,6 +80,8 @@
     y_recv,
     z_send,
     z_recv,
+    r_send,
+    r_recv,
 ):
     layers, rows, cols = sizes
     layer, row, col = (lax.axis_index(a) for a in ("layer", "row", "col"))
@@ -217,11 +224,11 @@
 
     @pl.when(layer == 0)
     def _():
-        z_in[0] = jnp.zeros_like(z_in[0])
+        z_in[0, 0] = jnp.zeros_like(z_in[0, 0])
 
     @pl.when(layer == last)
     def _():
-        z_in[layers] = jnp.zeros_like(z_in[layers])
+        z_in[layers, 0] = jnp.zeros_like(z_in[layers, 0])
 
     loads[5].wait()
 
@@ -287,13 +294,71 @@
                     cc * narrow : (cc + 1) * narrow
                 ]
             if a % per_half == per_half - 1:
-                for d in range(1, cols):
-                    y_copy(d, k, a // per_half).start()
+                sent(k, a // per_half)
+
+    end = jnp.logical_or(layer == 0, layer == last)
+    middle = jnp.logical_or(layer == layers // 2 - 1, layer == layers // 2)
+    onward = layer + 2 * flag(order[0] > layer) - 1
+
+    def sent(k, h):
+        if k == 0 and h == 0:
+
+            @pl.when(end)
+            def _():
+                for d in range(1, cols + 1):
+                    r_copy(d).start()
+
+        elif k < rows - 2:
+            exchange(k, h)
+        elif k == rows - 2 and h == halves - 1:
+            for other in reversed(range(1, halves)):
+                exchange(k, other)
+
+            @pl.when(jnp.logical_not(middle))
+            def _():
+                exchange(k, 0)
+
+        elif k == rows - 1:
+
+            @pl.when(jnp.logical_not(middle))
+            def _():
+                exchange(k, h)
+
+    def exchange(k, h):
+        for d in range(1, cols):
+            y_copy(d, k, h).start()
+
+    def r_copy(d):
+        cc = (col + d) % cols
+        return pltpu.make_async_remote_copy(
+            src_ref=packed.at[cc, 0, 0],
+            dst_ref=r_in.at[flag(middle), d - 1],
+            send_sem=r_send.at[d - 1],
+            recv_sem=r_recv.at[flag(middle), d - 1],
+            device_id={"layer": onward},
+            device_id_type=MESH,
+        )
+
+    def r_add(slot, k, d):
+        pltpu.make_async_remote_copy(
+            src_ref=packed.at[col, 0, 0],
+            dst_ref=r_in.at[slot, d - 1],
+            send_sem=r_send.at[d - 1],
+            recv_sem=r_recv.at[slot, d - 1],
+            device_id={"layer": onward},
+            device_id_type=MESH,
+        ).wait_recv()
+        cc = (col + d) % cols
+        value = packed[cc, k, 0].astype(F32) + r_in[slot, d - 1].astype(F32)
+        packed[cc, k, 0] = value.astype(BF16)
 
     def z_copy(k, h):
         j = order[k]
         toward = layer + 2 * flag(j > layer) - 1
         slot = j + flag(j == layer - 1) * (layers - j)
+        if k == 0:
+            toward = toward + flag(middle) * (j - toward)
+            slot = slot + flag(middle) * flag(j == last) * (layers - slot)
         return pltpu.make_async_remote_copy(
             src_ref=z_out.at[k, h],
             dst_ref=z_in.at[slot, h],
@@ -328,6 +393,8 @@
         passing = jnp.logical_or(
             jnp.logical_and(j > layer, layer > 0), jnp.logical_and(j < layer, layer < last)
         )
+        if k == rows - 2:
+            passing = jnp.logical_and(passing, jnp.logical_not(middle))
 
         with scope("z%d%d" % (k, h)):
 
@@ -350,23 +417,60 @@
             products(k)
 
     low_out[1] = x1[row].astype(F32).T.astype(BF16)
-    for k in range(rows - 1):
-        for h in range(halves):
+
+    with scope("rf"):
+
+        @pl.when(jnp.logical_not(end))
+        def _():
+            for d in range(1, cols + 1):
+                r_add(0, 0, d)
+                r_copy(d).start()
+
+    with scope("rn"):
+
+        @pl.when(middle)
+        def _():
+            for d in range(1, cols):
+                r_add(1, rows - 2, d)
+            exchange(rows - 2, 0)
+            for h in range(halves):
+                exchange(rows - 1, h)
+
+    for h in range(1, halves):
+        merge(0, h)
+
+    with scope("rw"):
+
+        @pl.when(middle)
+        def _():
+            r_add(1, rows - 2, cols)
+
+    before = [(k, h) for k in range(1, rows - 2) for h in range(halves)]
+    after = [(rows - 2, h) for h in reversed(range(halves))]
+
+    @pl.when(jnp.logical_not(middle))
+    def _():
+        for k, h in before + after:
+            merge(k, h)
+
+    @pl.when(middle)
+    def _():
+        for k, h in before[:-1] + after[:-1] + before[-1:] + after[-1:]:
             merge(k, h)
 
     loads[6].wait()
     loads[7].wait()
     with scope("zown"):
 
-        @pl.when(layer > 0)
-        def _():
-            for h in range(halves):
-                z_wait(layer, h)
-
-        @pl.when(layer < last)
-        def _():
-            for h in range(halves):
-                z_wait(layers, h)
+        for h in range(halves):
+            for slot, edge in ((layer, layer == 0), (layers, layer == last)):
+                if h:
+                    z_wait(slot, h)
+                else:
+
+                    @pl.when(jnp.logical_not(edge))
+                    def _():
+                        z_wait(slot, h)
 
     for h in range(halves):
         with scope("yown%d" % h):
@@ -394,10 +498,14 @@
             x_copy(m).wait_send()
         for k in range(rows):
             for h in range(halves):
+                if k == 0 and h == 0:
+                    continue
                 for d in range(1, cols):
                     y_copy(d, k, h).wait_send()
                 if k < rows - 1:
                     z_copy(k, h).wait_send()
+        for d in range(1, cols + 1):
+            r_copy(d).wait_send()
 
 
 def hand_over(low, anc, low_out, anc_out, sem):
@@ -417,7 +525,7 @@
     share = cases // rows
     halves = 2 if anc_row % 2 == 0 else 1
     chips = rows // 2
-    assert levels == 2 and layers == rows and rows % 2 == 0 and cols <= rows
+    assert levels == 2 and layers == rows and layers % 2 == 0 and layers > 3 and cols <= rows
     assert cols * narrow == share
     any_space = pl.BlockSpec(memory_space=pltpu.HBM)
     dma = pltpu.SemaphoreType.DMA
@@ -447,6 +555,7 @@
             pltpu.VMEM((cols - 1, rows, halves, narrow, wide), BF16),
             pltpu.VMEM((rows - 1, halves, narrow, wide), BF16),
             pltpu.VMEM((layers + 1, halves, narrow, wide), BF16),
+            pltpu.VMEM((2, cols, narrow, wide), BF16),
             pltpu.SMEM((levels, slots), jnp.int32),
             dma((9,)),
             dma((rows, chips)),
@@ -457,6 +566,8 @@
             dma((cols - 1, rows, halves)),
             dma((rows - 1, halves)),
             dma((layers + 1, halves)),
+            dma((cols,)),
+            dma((2, cols)),
         ],
         compiler_params=pltpu.CompilerParams(
             collective_id=0, has_side_effects=True, vmem_limit_bytes=56 * 1024 * 1024

time: 32.6 us -> 31 us (0.951)
  Pallas kernels: 31.8 us -> 30.2 us
    pallas_call x1, Pallas kernels: 31 us -> 29.4 us  [on_device(): pl.pallas_call(functools.partial(kernel, sizes), out_shape=(pltpu.VMEM((l...]
where the time goes in v2:
time: 31 us; the launch traced here: 30.9 us
  Pallas kernels  30.2 us (97%)
  between operations  0.64 us (2%)
    pallas_call x1, Pallas kernels, on_device(): pl.pallas_call(functools.partial(kernel, sizes), out_shape=(pltpu.VMEM((l...  29.4 us
    pallas_call x1, Pallas kernels, on_device(): pl.pallas_call(hand_over, out_shape=(jax.ShapeDtypeStruct(low.shape, low....  0.83 us

profile of v2, /device:TPU:0, one launch (start us, length us, event | category | flops | bytes accessed | tf_op | source)
XLA Modules:
  0.0 30.9 jit_solution(15220614277034905341)
XLA Ops:
  0.6 29.4 %shard_map.77 = (bf16[2,384,128]{2,1,0:T(8,128)(2,1)S(1)}, f32[4,64,384]{2,1,0:T(8,128)S(1)}) custom-call(s32[2,4]{1,0:T(2,128)} %bitcast.13, bf16[2,384,512]{2,1,0:T(8,128)(2,1)} %bitcast.10, bf16[2,384,384]{2,1,0:T(8,128)(2,1)} %bitcast.11, bf16[2,4,384,384]{3,2,1,0:T(8,128)(2,1)} %bitcast.9, bf16[4,64,384]{2,1,0:T(8,128)(2,1)} %bitcast.12, ...), custom_call_target="tpu_custom_call" | custom-call | tf_op jit(solution)/shard_map/pallas_call | solution.py:533
  30.0 0.8 %shard_map.78 = (bf16[2,384,128]{2,1,0:T(8,128)(2,1)}, f32[4,64,384]{2,1,0:T(8,128)}) custom-call(bf16[2,384,128]{2,1,0:T(8,128)(2,1)S(1)} %get-tuple-element.6.low, f32[4,64,384]{2,1,0:T(8,128)S(1)} %get-tuple-element.7.anc), custom_call_target="tpu_custom_call" | custom-call | tf_op jit(solution)/shard_map/pallas_call | solution.py:583

commit v3 on v1

v3 whole, which is shorter than its diff:
```python
import contextlib
import functools

import jax
import jax.numpy as jnp
from jax import lax
from jax.experimental import pallas as pl
from jax.experimental.pallas import tpu as pltpu
from jax.sharding import PartitionSpec as P

MESH = pl.DeviceIdType.MESH
F32 = jnp.float32
BF16 = jnp.bfloat16


def scope(name):
    return contextlib.nullcontext()


def dot_t(left, right):
    return lax.dot_general(left, right, (((1,), (1,)), ((), ())), preferred_element_type=F32)


def flag(condition):
    return condition.astype(jnp.int32)


def ranked(layer, layers):
    low = flag(layer < layers // 2)
    far, near = low * (layers - 1), (1 - low) * (layers - 1)
    keys = []
    for j in range(layers):
        key = -2 * layers * jnp.abs(layer - j) - j
        key = key - 1000 * layers * flag(far == j) + 1000 * layers * flag(near == j)
        keys.append(key + 5000 * layers * flag(layer == j))
    order = [0] * layers
    for j in range(layers):
        rank = 0
        for other in range(layers):
            if other != j:
                rank = rank + flag(keys[other] < keys[j])
        order = [order[k] + j * flag(rank == k) for k in range(layers)]
    return order


def kernel(
    sizes,
    targets_hbm,
    rhs_hbm,
    inv_hbm,
    blocks_hbm,
    rhs_anc_hbm,
    inv_anc_hbm,
    low_out,
    anc_out,
    rhs,
    inv,
    blocks0,
    blocks1,
    rhs_anc,
    inv_anc,
    x0,
    x1,
    part,
    part_in,
    rhs_t,
    base,
    packed,
    y_in,
    z_out,
    z_in,
    r_in,
    e_in,
    targets,
    load_sem,
    p_send,
    p_recv,
    x_send,
    x_recv,
    y_send,
    y_recv,
    z_send,
    z_recv,
    r_send,
    r_recv,
    e_send,
    e_recv,
):
    layers, rows, cols = sizes
    layer, row, col = (lax.axis_index(a) for a in ("layer", "row", "col"))
    slots = blocks0.shape[0]
    anc_row, narrow, width = rhs_anc.shape
    share = x1.shape[1]
    pieces = packed.shape[2]
    raw = pieces // 2
    chips = rows // 2
    last = layers - 1

    chip, core = row // 2, row % 2
    mate = row + 1 - 2 * core
    order = ranked(layer, layers)
    goal = (row + rows - 1) % rows
    active = goal < cols
    owner = (1 + col) % rows

    loads = [
        pltpu.make_async_copy(inv_hbm.at[0], inv.at[0], load_sem.at[0]),
        pltpu.make_async_copy(rhs_hbm.at[0], rhs.at[0], load_sem.at[1]),
        pltpu.make_async_copy(blocks_hbm.at[0], blocks0, load_sem.at[2]),
        pltpu.make_async_copy(inv_hbm.at[1], inv.at[1], load_sem.at[3]),
        pltpu.make_async_copy(rhs_hbm.at[1], rhs.at[1], load_sem.at[4]),
        pltpu.make_async_copy(blocks_hbm.at[1], blocks1, load_sem.at[5]),
        pltpu.make_async_copy(inv_anc_hbm, inv_anc, load_sem.at[6]),
        pltpu.make_async_copy(rhs_anc_hbm, rhs_anc, load_sem.at[7]),
        pltpu.make_async_copy(targets_hbm, targets, load_sem.at[8]),
    ]
    for n in (0, 1):
        loads[n].start()

    barrier = pltpu.get_barrier_semaphore()

    def greet(device):
        pl.semaphore_signal(barrier, inc=1, device_id=device, device_id_type=MESH)

    for d in range(1, rows):
        greet({"row": (row + d) % rows})
    for d in range(1, cols):
        greet({"col": (col + d) % cols})
    for step in (-1, 1):

        @pl.when(jnp.logical_and(layer + step >= 0, layer + step < layers))
        def _():
            greet({"layer": layer + step})

    for cc in range(cols):

        @pl.when(col != cc)
        def _():
            greet({"row": owner, "col": cc})

    @pl.when(jnp.logical_and(active, col != goal))
    def _():
        for r in range(rows):
            greet({"row": r, "col": goal})

    met = (rows - 1) + (cols - 1) + flag(layer > 0) + flag(layer < last)
    met = met + (cols - 1) + flag(jnp.logical_and(active, col != goal)) * rows

    for n in (8, 2, 3, 4, 5, 6, 7):
        loads[n].start()

    def listed(level, target):
        index, found = jnp.int32(0), jnp.int32(0)
        for s in range(slots):
            hit = (targets[level, s] == target).astype(jnp.int32)
            index = index + hit * s
            found = found + hit
        return (blocks0, blocks1)[level][index], found.astype(F32)

    def span(j):
        return pl.ds(pl.multiple_of(j * share, share), share)

    def solver(k, source):
        if k < 2:
            return [2 * ch + k for ch in range(chips)]
        return [2 * ((source // 2 + k - 2) % chips)]

    def place(k):
        return 0 if k < 2 else 1 + (k - 2) // chips

    def p_copy(k, n):
        return pltpu.make_async_remote_copy(
            src_ref=part.at[k],
            dst_ref=part_in.at[place(k), col],
            send_sem=p_send.at[k, n],
            recv_sem=p_recv.at[place(k), col],
            device_id={"row": solver(k, row)[n], "col": goal},
            device_id_type=MESH,
        )

    def here(k, n):
        return jnp.logical_and(goal == col, row == solver(k, row)[n])

    def part_of(k):
        block, found = listed(0, 1)
        part[k] = (dot_t(x0[span(order[k]), :], block) * found).astype(BF16)

    def part_out(k):
        for n in range(len(solver(k, row))):

            @pl.when(jnp.logical_not(here(k, n)))
            def _():
                p_copy(k, n).start()

            @pl.when(here(k, n))
            def _():
                part_in[place(k), col] = part[k]

    def lower(k):
        if share % 128 == 0:
            first = jnp.dot(inv[0], rhs[0, :, span(order[k])], preferred_element_type=F32)
            x0[span(order[k]), :] = first.T.astype(BF16)
        elif k == 0:
            first = jnp.dot(inv[0], rhs[0], preferred_element_type=F32)
            x0[...] = first.T.astype(BF16)

    with scope("ldx0"):
        loads[0].wait()
        loads[1].wait()
    with scope("x0"):
        lower(0)
    loads[8].wait()
    loads[2].wait()

    @pl.when(active)
    def _():
        part_of(0)

    with scope("barr"):
        pl.semaphore_wait(barrier, met)

    with scope("part"):

        @pl.when(active)
        def _():
            part_out(0)
            for k in range(1, rows):
                lower(k)
                part_of(k)
                part_out(k)

        @pl.when(jnp.logical_not(active))
        def _():
            for k in range(1, rows):
                lower(k)

    loads[3].wait()
    loads[4].wait()
    rhs_t[...] = rhs[1].astype(F32).T

    with scope("base"):
        for a in range(anc_row):
            block, found = listed(0, a + 2)
            base[:, a * width : (a + 1) * width] = dot_t(x0[...], block) * found

    for j in range(rows):

        @pl.when(row == j)
        def _():
            low_out[0] = x0[j * share : (j + 1) * share, :].astype(F32).T.astype(BF16)

    for edge, one, two in ((0, 0, layers), (last, layers, last)):

        @pl.when(layer == edge)
        def _():
            for h in range(pieces):
                if h < raw:
                    z_in[one, h] = jnp.zeros_like(z_in[one, h])
                elif layers == 4:
                    z_in[two, h] = jnp.zeros_like(z_in[two, h])

    loads[5].wait()

    def mate_copy(k):
        return pltpu.make_async_remote_copy(
            src_ref=x1.at[order[k]],
            dst_ref=x1.at[order[k]],
            send_sem=x_send.at[k, 0],
            recv_sem=x_recv.at[k],
            device_id={"row": mate},
            device_id_type=MESH,
        )

    def x_copy(k, d):
        return pltpu.make_async_remote_copy(
            src_ref=x1.at[order[k]],
            dst_ref=x1.at[order[k]],
            send_sem=x_send.at[k, d - 1],
            recv_sem=x_recv.at[k],
            device_id={"row": (row + d) % rows},
            device_id_type=MESH,
        )

    def solve(k):
        for cc in range(cols):

            @pl.when(jnp.logical_or(col != cc, row != owner))
            def _():
                pltpu.make_async_remote_copy(
                    src_ref=part.at[0],
                    dst_ref=part_in.at[place(k), cc],
                    send_sem=p_send.at[0, 0],
                    recv_sem=p_recv.at[place(k), cc],
                    device_id={"row": mate},
                    device_id_type=MESH,
                ).wait_recv()

        total = part_in[place(k), 0].astype(F32)
        for cc in range(1, cols):
            total = total + part_in[place(k), cc].astype(F32)
        residual = (rhs_t[span(order[k]), :] - total).astype(BF16)
        x1[order[k]] = dot_t(residual, inv[1]).astype(BF16)

    def solve_all(k):
        @pl.when(row == solver(k, owner)[0])
        def _():
            solve(k)
            for d in range(1, rows):
                x_copy(k, d).start()

    def y_copy(d, k, h):
        cc = (col + d) % cols
        return pltpu.make_async_remote_copy(
            src_ref=packed.at[cc, k, h],
            dst_ref=y_in.at[d - 1, k, h],
            send_sem=y_send.at[d - 1, k, h],
            recv_sem=y_recv.at[d - 1, k, h],
            device_id={"col": cc},
            device_id_type=MESH,
        )

    def products(k):
        @pl.when(core != k if k < 2 else row != solver(k, owner)[0])
        def _():
            mate_copy(k).wait_recv()

        j = order[k]
        for a in range(anc_row):
            block, found = listed(1, a + 2)
            at = slice(a * width, (a + 1) * width)
            value = base[span(j), at] + dot_t(x1[j], block) * found
            value = value.astype(BF16)
            for cc in range(cols):
                packed[cc, k, a] = value[cc * narrow : (cc + 1) * narrow]
            sent(k, a)

    end = jnp.logical_or(layer == 0, layer == last)
    middle = jnp.logical_or(layer == layers // 2 - 1, layer == layers // 2)
    upper = layer == layers // 2
    beside = jnp.logical_or(layer == layers // 2 - 2, layer == layers // 2 + 1)
    onward = layer + 2 * flag(order[0] > layer) - 1

    others, whole = range(1, cols), range(1, cols + 1)

    def sent(k, h):
        if k == 0 and h < raw:

            @pl.when(end)
            def _():
                for d in others:
                    r_copy(d, h).start()
                if h == raw - 1:
                    for n in range(raw):
                        r_copy(cols, n).start()

        elif k == rows - 2 and h >= raw:

            @pl.when(middle)
            def _():
                for d in others:
                    e_copy(d, h).start()
                if h == pieces - 1:
                    for n in range(raw, pieces):
                        e_copy(cols, n).start()

            @pl.when(jnp.logical_not(middle))
            def _():
                exchange(k, h)

        elif k == rows - 2:

            @pl.when(jnp.logical_not(middle))
            def _():
                exchange(k, h)

        elif k == rows - 1:

            @pl.when(jnp.logical_not(jnp.logical_or(middle, end) if h >= raw else middle))
            def _():
                exchange(k, h)

        else:
            exchange(k, h)

    def exchange(k, h):
        for d in range(1, cols):
            y_copy(d, k, h).start()

    def r_copy(d, h):
        cc = (col + d) % cols
        return pltpu.make_async_remote_copy(
            src_ref=packed.at[cc, 0, h],
            dst_ref=r_in.at[flag(middle), d - 1, h],
            send_sem=r_send.at[d - 1, h],
            recv_sem=r_recv.at[flag(middle), d - 1, h],
            device_id={"layer": onward},
            device_id_type=MESH,
        )

    def r_add(slot, k, d, h):
        pltpu.make_async_remote_copy(
            src_ref=packed.at[col, 0, h],
            dst_ref=r_in.at[slot, d - 1, h],
            send_sem=r_send.at[d - 1, h],
            recv_sem=r_recv.at[slot, d - 1, h],
            device_id={"layer": onward},
            device_id_type=MESH,
        ).wait_recv()
        cc = (col + d) % cols
        value = packed[cc, k, h].astype(F32) + r_in[slot, d - 1, h].astype(F32)
        packed[cc, k, h] = value.astype(BF16)

    def e_copy(d, h):
        cc = (col + d) % cols
        return pltpu.make_async_remote_copy(
            src_ref=packed.at[cc, rows - 2, h],
            dst_ref=e_in.at[d - 1, h - raw],
            send_sem=e_send.at[d - 1, h - raw],
            recv_sem=e_recv.at[d - 1, h - raw],
            device_id={"layer": order[rows - 2]},
            device_id_type=MESH,
        )

    def e_add(d, h):
        e_copy(d, h).wait_recv()
        cc = (col + d) % cols
        value = packed[cc, rows - 1, h].astype(F32) + e_in[d - 1, h - raw].astype(F32)
        packed[cc, rows - 1, h] = value.astype(BF16)

    def z_copy(k, h):
        j = order[k]
        toward = layer + 2 * flag(j > layer) - 1
        slot = j + flag(j == layer - 1) * (layers - j)
        if k == 0:
            toward = toward + flag(middle) * (j - toward)
            slot = slot + flag(middle) * flag(j == last) * (layers - slot)
        return pltpu.make_async_remote_copy(
            src_ref=z_out.at[k, h],
            dst_ref=z_in.at[slot, h],
            send_sem=z_send.at[k, h],
            recv_sem=z_recv.at[slot, h],
            device_id={"layer": toward},
            device_id_type=MESH,
        )

    def z_wait(slot, h):
        pltpu.make_async_remote_copy(
            src_ref=z_out.at[0, h],
            dst_ref=z_in.at[slot, h],
            send_sem=z_send.at[0, h],
            recv_sem=z_recv.at[slot, h],
            device_id={"layer": (layer + 1) % layers},
            device_id_type=MESH,
        ).wait_recv()

    def merged(k, h):
        for d in range(1, cols):
            y_copy(d, k, h).wait_recv()
        value = packed[col, k, h].astype(F32)
        for d in range(1, cols):
            value = value + y_in[d - 1, k, h].astype(F32)
        return value

    def merge(k, h):
        with scope("y%d%d" % (k, h)):
            value = merged(k, h)
        j = order[k]
        passing = jnp.logical_or(
            jnp.logical_and(j > layer, layer > 0), jnp.logical_and(j < layer, layer < last)
        )
        if k == rows - 2:
            passing = jnp.logical_and(passing, jnp.logical_not(middle))
            if h >= raw:
                passing = jnp.logical_and(passing, jnp.logical_not(beside))

        with scope("z%d%d" % (k, h)):

            @pl.when(passing)
            def _():
                z_wait(j, h)
                z_out[k, h] = (value + z_in[j, h].astype(F32)).astype(BF16)

            @pl.when(jnp.logical_not(passing))
            def _():
                z_out[k, h] = value.astype(BF16)

        z_copy(k, h).start()

    for k in range(2):

        @pl.when(core == k)
        def _():
            with scope("x1"):
                solve(k)
            mate_copy(k).start()

    first = [(0, h) for h in range(raw, pieces)]
    early = [(k, h) for k in range(1, rows - 2) for h in range(pieces)]
    late = [(rows - 2, h) for h in range(pieces)]

    for k in range(rows):
        with scope("p%d" % k):
            products(k)
        if k == 0:
            with scope("x1_2"):
                solve_all(2)
        elif k == 1:
            with scope("x1_3"):
                for other in range(3, rows):
                    solve_all(other)

            @pl.when(jnp.logical_not(end))
            def _():
                with scope("rf1"):
                    for h in range(raw):
                        for d in others:
                            r_add(0, 0, d, h)
                            r_copy(d, h).start()

        elif k == 2:

            @pl.when(end)
            def _():
                for k, h in first:
                    merge(k, h)

            @pl.when(jnp.logical_not(end))
            def _():
                with scope("rf2"):
                    for h in range(raw):
                        r_add(0, 0, cols, h)
                        r_copy(cols, h).start()

    low_out[1] = x1[row].astype(F32).T.astype(BF16)

    @pl.when(middle)
    def _():
        with scope("rn"):
            for h in range(raw):
                for d in others:
                    r_add(1, rows - 2, d, h)
                exchange(rows - 2, h)
            for h in range(pieces):
                exchange(rows - 1, h)

        for k, h in first:
            merge(k, h)

        with scope("rw"):
            for h in range(raw):
                r_add(1, rows - 2, cols, h)

        near = late[:raw]

        @pl.when(upper)
        def _():
            for k, h in early[:-2] + near + early[-2:]:
                merge(k, h)

        @pl.when(jnp.logical_not(upper))
        def _():
            for k, h in early[:-1] + near[:1] + early[-1:] + near[1:]:
                merge(k, h)

    @pl.when(jnp.logical_not(middle))
    def _():
        @pl.when(jnp.logical_not(end))
        def _():
            for k, h in first:
                merge(k, h)

        for k, h in early + late[:raw]:
            merge(k, h)

        with scope("e"):

            @pl.when(end)
            def _():
                for h in range(raw, pieces):
                    for d in others:
                        e_add(d, h)
                    exchange(rows - 1, h)
                for h in range(raw, pieces):
                    e_add(cols, h)

        for k, h in late[raw:]:
            merge(k, h)

    loads[6].wait()
    loads[7].wait()
    for h in range(pieces):
        with scope("zown%d" % h):
            for slot, edge, far in ((layer, 0, last), (layers, last, 0)):
                if h < raw:

                    @pl.when(layer != edge)
                    def _():
                        z_wait(slot, h)

                elif layers == 4:

                    @pl.when(layer != far)
                    def _():
                        z_wait(slot, h)

                else:
                    z_wait(slot, h)

        with scope("yown%d" % h):
            value = merged(rows - 1, h)
        with scope("fin%d" % h):
            value = value + z_in[layer, h].astype(F32) + z_in[layers, h].astype(F32)
            residual = (rhs_anc[h].astype(F32) - value).astype(BF16)
            anc_out[h] = dot_t(residual, inv_anc[h])

    with scope("sent"):

        @pl.when(active)
        def _():
            for k in range(rows):
                for n in range(len(solver(k, row))):

                    @pl.when(jnp.logical_not(here(k, n)))
                    def _():
                        p_copy(k, n).wait_send()

        for k in range(2):

            @pl.when(core == k)
            def _():
                mate_copy(k).wait_send()

        for k in range(2, rows):

            @pl.when(row == solver(k, owner)[0])
            def _():
                for d in range(1, rows):
                    x_copy(k, d).wait_send()

        for k in range(rows):
            for h in range(pieces):
                if k == 0 and h < raw or k == rows - 2 and h >= raw:
                    continue
                for d in others:
                    y_copy(d, k, h).wait_send()
                if k < rows - 1:
                    z_copy(k, h).wait_send()
        for d in whole:
            for h in range(raw):
                r_copy(d, h).wait_send()

        for h in range(raw, pieces):

            @pl.when(middle)
            def _():
                for d in whole:
                    e_copy(d, h).wait_send()

            @pl.when(jnp.logical_not(middle))
            def _():
                for d in others:
                    y_copy(d, rows - 2, h).wait_send()
                z_copy(rows - 2, h).wait_send()


def hand_over(low, anc, low_out, anc_out, sem):
    first = pltpu.make_async_copy(anc, anc_out, sem.at[0])
    second = pltpu.make_async_copy(low, low_out, sem.at[1])
    first.start()
    second.start()
    first.wait()
    second.wait()


def on_device(sizes, rhs_low, inv_low, blocks, targets, rhs_anc, inv_anc):
    layers, rows, cols = sizes
    levels, slots = blocks.shape[3], blocks.shape[4]
    width, cases = rhs_low.shape[3], rhs_low.shape[4]
    anc_row, narrow = rhs_anc.shape[0], rhs_anc.shape[2]
    share = cases // rows
    pieces, raw = anc_row, anc_row // 2
    chips = rows // 2
    places = 1 + pl.cdiv(rows - 2, chips)
    assert levels == 2 and layers == rows and layers % 2 == 0 and layers > 3 and cols <= rows
    assert cols * narrow == share and anc_row % 2 == 0
    any_space = pl.BlockSpec(memory_space=pltpu.HBM)
    dma = pltpu.SemaphoreType.DMA
    low, anc = pl.pallas_call(
        functools.partial(kernel, sizes),
        out_shape=(
            pltpu.VMEM((levels, width, share), BF16),
            pltpu.VMEM((anc_row, narrow, width), F32),
        ),
        in_specs=[any_space] * 6,
        out_specs=(pl.BlockSpec(memory_space=pltpu.VMEM), pl.BlockSpec(memory_space=pltpu.VMEM)),
        scratch_shapes=[
            pltpu.VMEM((levels, width, cases), BF16),
            pltpu.VMEM((levels, width, width), BF16),
            pltpu.VMEM((slots, width, width), BF16),
            pltpu.VMEM((slots, width, width), BF16),
            pltpu.VMEM((anc_row, narrow, width), BF16),
            pltpu.VMEM((anc_row, width, width), BF16),
            pltpu.VMEM((cases, width), BF16),
            pltpu.VMEM((rows, share, width), BF16),
            pltpu.VMEM((rows, share, width), BF16),
            pltpu.VMEM((places, cols, share, width), BF16),
            pltpu.VMEM((cases, width), F32),
            pltpu.VMEM((cases, anc_row * width), F32),
            pltpu.VMEM((cols, rows, pieces, narrow, width), BF16),
            pltpu.VMEM((cols - 1, rows, pieces, narrow, width), BF16),
            pltpu.VMEM((rows - 1, pieces, narrow, width), BF16),
            pltpu.VMEM((layers + 1, pieces, narrow, width), BF16),
            pltpu.VMEM((2, cols, raw, narrow, width), BF16),
            pltpu.VMEM((cols, pieces - raw, narrow, width), BF16),
            pltpu.SMEM((levels, slots), jnp.int32),
            dma((9,)),
            dma((rows, chips)),
            dma((places, cols)),
            dma((rows, rows - 1)),
            dma((rows,)),
            dma((cols - 1, rows, pieces)),
            dma((cols - 1, rows, pieces)),
            dma((rows - 1, pieces)),
            dma((layers + 1, pieces)),
            dma((cols, raw)),
            dma((2, cols, raw)),
            dma((cols, pieces - raw)),
            dma((cols, pieces - raw)),
        ],
        compiler_params=pltpu.CompilerParams(
            collective_id=0, has_side_effects=True, vmem_limit_bytes=56 * 1024 * 1024
        ),
    )(
        targets.reshape(levels, slots),
        rhs_low.reshape(levels, width, cases),
        inv_low.reshape(levels, width, width),
        blocks.reshape(levels, slots, width, width),
        rhs_anc.transpose(0, 2, 1),
        inv_anc,
    )
    low, anc = pl.pallas_call(
        hand_over,
        out_shape=(
            jax.ShapeDtypeStruct(low.shape, low.dtype),
            jax.ShapeDtypeStruct(anc.shape, anc.dtype),
        ),
        in_specs=[pl.BlockSpec(memory_space=pltpu.VMEM)] * 2,
        out_specs=(any_space, any_space),
        scratch_shapes=[dma((2,))],
        compiler_params=pltpu.CompilerParams(vmem_limit_bytes=4 * 1024 * 1024),
    )(low, anc)
    return low[None, :, None], anc.transpose(0, 2, 1)


def solution(mesh):
    sizes = tuple(mesh.shape[a] for a in ("layer", "row", "col"))
    in_specs = (
        P("layer", None, "col", None, None),
        P("layer", None, "col", None, None),
        P("layer", "row", "col", None, None, None, None),
        P("layer", "row", "col", None, None),
        P("row", None, ("layer", "col")),
        P("row", None, None),
    )
    out_specs = (P("layer", None, "col", None, "row"), P("row", None, ("layer", "col")))
    return jax.shard_map(
        functools.partial(on_device, sizes),
        mesh=mesh,
        in_specs=in_specs,
        out_specs=out_specs,
        check_vma=False,
    )
```

time: 32.6 us -> 29.1 us (0.89)
  the two profiles are of different devices: /device:TPU:0 before, /device:TPU:21 now
where the time goes in v3:
time: 29.1 us; the launch traced here: 28.9 us
  Pallas kernels  28.3 us (97%)
  between operations  0.64 us (2%)
    pallas_call x1, Pallas kernels, on_device(): pl.pallas_call(functools.partial(kernel, sizes), out_shape=(pltpu.VMEM((l...  27.4 us
    pallas_call x1, Pallas kernels, on_device(): pl.pallas_call(hand_over, out_shape=(jax.ShapeDtypeStruct(low.shape, low....  0.83 us

profile of v3, /device:TPU:21, one launch (start us, length us, event | category | flops | bytes accessed | tf_op | source)
XLA Modules:
  0.0 28.9 jit_solution(11899722978120225917)
XLA Ops:
  0.6 27.4 %shard_map.77 = (bf16[2,384,128]{2,1,0:T(8,128)(2,1)S(1)}, f32[4,64,384]{2,1,0:T(8,128)S(1)}) custom-call(s32[2,4]{1,0:T(2,128)} %bitcast.13, bf16[2,384,512]{2,1,0:T(8,128)(2,1)} %bitcast.10, bf16[2,384,384]{2,1,0:T(8,128)(2,1)} %bitcast.11, bf16[2,4,384,384]{3,2,1,0:T(8,128)(2,1)} %bitcast.9, bf16[4,64,384]{2,1,0:T(8,128)(2,1)} %bitcast.12, ...), custom_call_target="tpu_custom_call" | custom-call | tf_op jit(solution)/shard_map/pallas_call | solution.py:688
  28.1 0.8 %shard_map.78 = (bf16[2,384,128]{2,1,0:T(8,128)(2,1)}, f32[4,64,384]{2,1,0:T(8,128)}) custom-call(bf16[2,384,128]{2,1,0:T(8,128)(2,1)S(1)} %get-tuple-element.6.low, f32[4,64,384]{2,1,0:T(8,128)S(1)} %get-tuple-element.7.anc), custom_call_target="tpu_custom_call" | custom-call | tf_op jit(solution)/shard_map/pallas_call | solution.py:741

commit v4 on v3

--- a/solution.py
+++ b/solution.py
@@ -77,21 +77,18 @@
     p_recv,
     x_send,
     x_recv,
-    y_send,
     y_recv,
-    z_send,
     z_recv,
-    r_send,
     r_recv,
-    e_send,
     e_recv,
+    send_sem,
 ):
     layers, rows, cols = sizes
     layer, row, col = (lax.axis_index(a) for a in ("layer", "row", "col"))
     slots = blocks0.shape[0]
     anc_row, narrow, width = rhs_anc.shape
     share = x1.shape[1]
-    pieces = packed.shape[2]
+    pieces = anc_row
     raw = pieces // 2
     chips = rows // 2
     last = layers - 1
@@ -149,6 +146,22 @@
     for n in (8, 2, 3, 4, 5, 6, 7):
         loads[n].start()
 
+    def spare(j):
+        return (1 - j % 2) * last if layers == 4 else layers
+
+    def at(cc, k, h):
+        return (cc * rows + k) * pieces + h
+
+    def sends(n):
+        return pltpu.make_async_remote_copy(
+            src_ref=packed.at[0:n],
+            dst_ref=packed.at[0:n],
+            send_sem=send_sem,
+            recv_sem=send_sem,
+            device_id={"row": mate},
+            device_id_type=MESH,
+        )
+
     def listed(level, target):
         index, found = jnp.int32(0), jnp.int32(0)
         for s in range(slots):
@@ -172,7 +185,7 @@
         return pltpu.make_async_remote_copy(
             src_ref=part.at[k],
             dst_ref=part_in.at[place(k), col],
-            send_sem=p_send.at[k, n],
+            send_sem=p_send,
             recv_sem=p_recv.at[place(k), col],
             device_id={"row": solver(k, row)[n], "col": goal},
             device_id_type=MESH,
@@ -249,7 +262,7 @@
         def _():
             low_out[0] = x0[j * share : (j + 1) * share, :].astype(F32).T.astype(BF16)
 
-    for edge, one, two in ((0, 0, layers), (last, layers, last)):
+    for edge, one, two in ((0, 0, spare(0)), (last, spare(last), last)):
 
         @pl.when(layer == edge)
         def _():
@@ -265,7 +278,7 @@
         return pltpu.make_async_remote_copy(
             src_ref=x1.at[order[k]],
             dst_ref=x1.at[order[k]],
-            send_sem=x_send.at[k, 0],
+            send_sem=x_send.at[0],
             recv_sem=x_recv.at[k],
             device_id={"row": mate},
             device_id_type=MESH,
@@ -275,11 +288,31 @@
         return pltpu.make_async_remote_copy(
             src_ref=x1.at[order[k]],
             dst_ref=x1.at[order[k]],
-            send_sem=x_send.at[k, d - 1],
+            send_sem=x_send.at[k - 1],
             recv_sem=x_recv.at[k],
             device_id={"row": (row + d) % rows},
             device_id_type=MESH,
         )
+
+    def p_sent(n):
+        pltpu.make_async_remote_copy(
+            src_ref=packed.at[0 : n * cols],
+            dst_ref=packed.at[0 : n * cols],
+            send_sem=p_send,
+            recv_sem=p_send,
+            device_id={"row": mate},
+            device_id_type=MESH,
+        ).wait_send()
+
+    def x_sent(k):
+        pltpu.make_async_remote_copy(
+            src_ref=x1.at[0 : rows - 1],
+            dst_ref=x1.at[0 : rows - 1],
+            send_sem=x_send.at[k - 1],
+            recv_sem=x_send.at[k - 1],
+            device_id={"row": mate},
+            device_id_type=MESH,
+        ).wait_send()
 
     def solve(k):
         for cc in range(cols):
@@ -289,7 +322,7 @@
                 pltpu.make_async_remote_copy(
                     src_ref=part.at[0],
                     dst_ref=part_in.at[place(k), cc],
-                    send_sem=p_send.at[0, 0],
+                    send_sem=p_send,
                     recv_sem=p_recv.at[place(k), cc],
                     device_id={"row": mate},
                     device_id_type=MESH,
@@ -311,13 +344,17 @@
     def y_copy(d, k, h):
         cc = (col + d) % cols
         return pltpu.make_async_remote_copy(
-            src_ref=packed.at[cc, k, h],
+            src_ref=packed.at[at(cc, k, h)],
             dst_ref=y_in.at[d - 1, k, h],
-            send_sem=y_send.at[d - 1, k, h],
-            recv_sem=y_recv.at[d - 1, k, h],
+            send_sem=send_sem,
+            recv_sem=y_recv.at[d - 1, k * pieces + h - raw],
             device_id={"col": cc},
             device_id_type=MESH,
         )
+
+    others, whole = range(1, cols), range(1, cols + 1)
+    mixed = [(h, h + raw) for h in range(raw)]
+    plain = [(2 * h, 2 * h + 1) for h in range(raw)]
 
     def products(k):
         @pl.when(core != k if k < 2 else row != solver(k, owner)[0])
@@ -325,14 +362,16 @@
             mate_copy(k).wait_recv()
 
         j = order[k]
-        for a in range(anc_row):
-            block, found = listed(1, a + 2)
-            at = slice(a * width, (a + 1) * width)
-            value = base[span(j), at] + dot_t(x1[j], block) * found
-            value = value.astype(BF16)
-            for cc in range(cols):
-                packed[cc, k, a] = value[cc * narrow : (cc + 1) * narrow]
-            sent(k, a)
+        for pair in plain if k else mixed:
+            for a in pair:
+                block, found = listed(1, a + 2)
+                lanes = slice(a * width, (a + 1) * width)
+                value = base[span(j), lanes] + dot_t(x1[j], block) * found
+                value = value.astype(BF16)
+                for cc in range(cols):
+                    packed[at(cc, k, a)] = value[cc * narrow : (cc + 1) * narrow]
+            for a in pair:
+                sent(k, a)
 
     end = jnp.logical_or(layer == 0, layer == last)
     middle = jnp.logical_or(layer == layers // 2 - 1, layer == layers // 2)
@@ -340,7 +379,6 @@
     beside = jnp.logical_or(layer == layers // 2 - 2, layer == layers // 2 + 1)
     onward = layer + 2 * flag(order[0] > layer) - 1
 
-    others, whole = range(1, cols), range(1, cols + 1)
 
     def sent(k, h):
         if k == 0 and h < raw:
@@ -375,9 +413,13 @@
 
         elif k == rows - 1:
 
-            @pl.when(jnp.logical_not(jnp.logical_or(middle, end) if h >= raw else middle))
-            def _():
+            if h < raw:
                 exchange(k, h)
+            else:
+
+                @pl.when(jnp.logical_not(end))
+                def _():
+                    exchange(k, h)
 
         else:
             exchange(k, h)
@@ -386,58 +428,81 @@
         for d in range(1, cols):
             y_copy(d, k, h).start()
 
+    def r_place(d, h):
+        return (d - 1) * raw + h if d < cols else (cols - 1) * raw
+
+    def e_place(d, h):
+        return (d - 1) * (pieces - raw) + h - raw if d < cols else (cols - 1) * (pieces - raw)
+
     def r_copy(d, h):
         cc = (col + d) % cols
         return pltpu.make_async_remote_copy(
-            src_ref=packed.at[cc, 0, h],
+            src_ref=packed.at[at(cc, 0, h)],
             dst_ref=r_in.at[flag(middle), d - 1, h],
-            send_sem=r_send.at[d - 1, h],
-            recv_sem=r_recv.at[flag(middle), d - 1, h],
+            send_sem=send_sem,
+            recv_sem=r_recv.at[flag(middle), r_place(d, h)],
             device_id={"layer": onward},
             device_id_type=MESH,
         )
 
+    def r_wait(slot, d, h):
+        own = d == cols
+        pltpu.make_async_remote_copy(
+            src_ref=r_in.at[slot, d - 1] if own else r_in.at[slot, d - 1, h],
+            dst_ref=r_in.at[slot, d - 1] if own else r_in.at[slot, d - 1, h],
+            send_sem=send_sem,
+            recv_sem=r_recv.at[slot, r_place(d, h)],
+            device_id={"layer": onward},
+            device_id_type=MESH,
+        ).wait_recv()
+
     def r_add(slot, k, d, h):
-        pltpu.make_async_remote_copy(
-            src_ref=packed.at[col, 0, h],
-            dst_ref=r_in.at[slot, d - 1, h],
-            send_sem=r_send.at[d - 1, h],
-            recv_sem=r_recv.at[slot, d - 1, h],
-            device_id={"layer": onward},
-            device_id_type=MESH,
-        ).wait_recv()
+        if d < cols or h == 0:
+            r_wait(slot, d, h)
         cc = (col + d) % cols
-        value = packed[cc, k, h].astype(F32) + r_in[slot, d - 1, h].astype(F32)
-        packed[cc, k, h] = value.astype(BF16)
+        value = packed[at(cc, k, h)].astype(F32) + r_in[slot, d - 1, h].astype(F32)
+        packed[at(cc, k, h)] = value.astype(BF16)
 
     def e_copy(d, h):
         cc = (col + d) % cols
         return pltpu.make_async_remote_copy(
-            src_ref=packed.at[cc, rows - 2, h],
+            src_ref=packed.at[at(cc, rows - 2, h)],
             dst_ref=e_in.at[d - 1, h - raw],
-            send_sem=e_send.at[d - 1, h - raw],
-            recv_sem=e_recv.at[d - 1, h - raw],
+            send_sem=send_sem,
+            recv_sem=e_recv.at[e_place(d, h)],
             device_id={"layer": order[rows - 2]},
             device_id_type=MESH,
         )
 
     def e_add(d, h):
-        e_copy(d, h).wait_recv()
+        if d < cols:
+            e_copy(d, h).wait_recv()
+        elif h == raw:
+            pltpu.make_async_remote_copy(
+                src_ref=e_in.at[d - 1],
+                dst_ref=e_in.at[d - 1],
+                send_sem=send_sem,
+                recv_sem=e_recv.at[e_place(d, h)],
+                device_id={"layer": onward},
+                device_id_type=MESH,
+            ).wait_recv()
         cc = (col + d) % cols
-        value = packed[cc, rows - 1, h].astype(F32) + e_in[d - 1, h - raw].astype(F32)
-        packed[cc, rows - 1, h] = value.astype(BF16)
+        value = packed[at(cc, rows - 1, h)].astype(F32) + e_in[d - 1, h - raw].astype(F32)
+        packed[at(cc, rows - 1, h)] = value.astype(BF16)
 
     def z_copy(k, h):
         j = order[k]
         toward = layer + 2 * flag(j > layer) - 1
-        slot = j + flag(j == layer - 1) * (layers - j)
         if k == 0:
             toward = toward + flag(middle) * (j - toward)
-            slot = slot + flag(middle) * flag(j == last) * (layers - slot)
+        other = jnp.logical_and(j == toward, j < layer)
+        if k == 0:
+            other = jnp.logical_and(j == toward, jnp.logical_xor(j < layer, middle))
+        slot = j + flag(other) * (spare(j) - j)
         return pltpu.make_async_remote_copy(
             src_ref=z_out.at[k, h],
             dst_ref=z_in.at[slot, h],
-            send_sem=z_send.at[k, h],
+            send_sem=send_sem,
             recv_sem=z_recv.at[slot, h],
             device_id={"layer": toward},
             device_id_type=MESH,
@@ -447,7 +512,7 @@
         pltpu.make_async_remote_copy(
             src_ref=z_out.at[0, h],
             dst_ref=z_in.at[slot, h],
-            send_sem=z_send.at[0, h],
+            send_sem=send_sem,
             recv_sem=z_recv.at[slot, h],
             device_id={"layer": (layer + 1) % layers},
             device_id_type=MESH,
@@ -456,7 +521,7 @@
     def merged(k, h):
         for d in range(1, cols):
             y_copy(d, k, h).wait_recv()
-        value = packed[col, k, h].astype(F32)
+        value = packed[at(col, k, h)].astype(F32)
         for d in range(1, cols):
             value = value + y_in[d - 1, k, h].astype(F32)
         return value
@@ -498,40 +563,40 @@
     early = [(k, h) for k in range(1, rows - 2) for h in range(pieces)]
     late = [(rows - 2, h) for h in range(pieces)]
 
-    for k in range(rows):
+    def step(k):
         with scope("p%d" % k):
             products(k)
-        if k == 0:
-            with scope("x1_2"):
-                solve_all(2)
-        elif k == 1:
-            with scope("x1_3"):
-                for other in range(3, rows):
-                    solve_all(other)
-
-            @pl.when(jnp.logical_not(end))
-            def _():
-                with scope("rf1"):
-                    for h in range(raw):
-                        for d in others:
-                            r_add(0, 0, d, h)
-                            r_copy(d, h).start()
-
-        elif k == 2:
-
-            @pl.when(end)
-            def _():
-                for k, h in first:
-                    merge(k, h)
-
-            @pl.when(jnp.logical_not(end))
-            def _():
-                with scope("rf2"):
-                    for h in range(raw):
-                        r_add(0, 0, cols, h)
-                        r_copy(cols, h).start()
-
-    low_out[1] = x1[row].astype(F32).T.astype(BF16)
+
+    step(0)
+    with scope("x1_2"):
+        solve_all(2)
+    step(1)
+    with scope("x1_3"):
+        for k in range(3, rows):
+            solve_all(k)
+
+    @pl.when(jnp.logical_not(end))
+    def _():
+        with scope("rf1"):
+            for h in range(raw):
+                for d in others:
+                    r_add(0, 0, d, h)
+                    r_copy(d, h).start()
+
+    for k in range(2, rows - 1):
+        step(k)
+
+    @pl.when(end)
+    def _():
+        for k, h in first + early[:raw]:
+            merge(k, h)
+
+    @pl.when(jnp.logical_not(end))
+    def _():
+        with scope("rf2"):
+            for h in range(raw):
+                r_add(0, 0, cols, h)
+                r_copy(cols, h).start()
 
     @pl.when(middle)
     def _():
@@ -540,9 +605,12 @@
                 for d in others:
                     r_add(1, rows - 2, d, h)
                 exchange(rows - 2, h)
-            for h in range(pieces):
-                exchange(rows - 1, h)
-
+
+    step(rows - 1)
+    low_out[1] = x1[row].astype(F32).T.astype(BF16)
+
+    @pl.when(middle)
+    def _():
         for k, h in first:
             merge(k, h)
 
@@ -559,7 +627,7 @@
 
         @pl.when(jnp.logical_not(upper))
         def _():
-            for k, h in early[:-1] + near[:1] + early[-1:] + near[1:]:
+            for k, h in early[:raw] + near[:1] + early[raw:-1] + near[1:] + early[-1:]:
                 merge(k, h)
 
     @pl.when(jnp.logical_not(middle))
@@ -569,7 +637,12 @@
             for k, h in first:
                 merge(k, h)
 
-        for k, h in early + late[:raw]:
+        @pl.when(jnp.logical_not(end))
+        def _():
+            for k, h in early[:raw]:
+                merge(k, h)
+
+        for k, h in early[raw:] + late[:raw]:
             merge(k, h)
 
         with scope("e"):
@@ -590,7 +663,7 @@
     loads[7].wait()
     for h in range(pieces):
         with scope("zown%d" % h):
-            for slot, edge, far in ((layer, 0, last), (layers, last, 0)):
+            for slot, edge, far in ((layer, 0, last), (spare(layer), last, 0)):
                 if h < raw:
 
                     @pl.when(layer != edge)
@@ -609,58 +682,40 @@
         with scope("yown%d" % h):
             value = merged(rows - 1, h)
         with scope("fin%d" % h):
-            value = value + z_in[layer, h].astype(F32) + z_in[layers, h].astype(F32)
+            value = value + z_in[layer, h].astype(F32) + z_in[spare(layer), h].astype(F32)
             residual = (rhs_anc[h].astype(F32) - value).astype(BF16)
             anc_out[h] = dot_t(residual, inv_anc[h])
 
     with scope("sent"):
-
-        @pl.when(active)
-        def _():
-            for k in range(rows):
-                for n in range(len(solver(k, row))):
-
-                    @pl.when(jnp.logical_not(here(k, n)))
-                    def _():
-                        p_copy(k, n).wait_send()
-
-        for k in range(2):
-
-            @pl.when(core == k)
-            def _():
-                mate_copy(k).wait_send()
-
+        total = 2 * chips + rows - 2
+        mine = goal == col
+        for n, case in (
+            (total, jnp.logical_not(mine)),
+            (total - 2, jnp.logical_and(mine, core == 0)),
+            (total - 1, jnp.logical_and(mine, core == 1)),
+        ):
+
+            @pl.when(jnp.logical_and(active, case))
+            def _():
+                p_sent(n)
+
+        mate_copy(0).wait_send()
         for k in range(2, rows):
 
             @pl.when(row == solver(k, owner)[0])
             def _():
-                for d in range(1, rows):
-                    x_copy(k, d).wait_send()
-
-        for k in range(rows):
-            for h in range(pieces):
-                if k == 0 and h < raw or k == rows - 2 and h >= raw:
-                    continue
-                for d in others:
-                    y_copy(d, k, h).wait_send()
-                if k < rows - 1:
-                    z_copy(k, h).wait_send()
-        for d in whole:
-            for h in range(raw):
-                r_copy(d, h).wait_send()
-
-        for h in range(raw, pieces):
-
-            @pl.when(middle)
-            def _():
-                for d in whole:
-                    e_copy(d, h).wait_send()
-
-            @pl.when(jnp.logical_not(middle))
-            def _():
-                for d in others:
-                    y_copy(d, rows - 2, h).wait_send()
-                z_copy(rows - 2, h).wait_send()
+                x_sent(k)
+
+        far, every = raw * cols, pieces * (cols - 1)
+        kept = (pieces - raw) * (cols - 1) + every * (rows - 2) + (pieces - raw) + pieces * (rows - 3)
+
+        @pl.when(middle)
+        def _():
+            sends(far + kept + raw * (cols - 1) + raw + (pieces - raw) * cols).wait_send()
+
+        @pl.when(jnp.logical_not(middle))
+        def _():
+            sends(far + kept + every + pieces).wait_send()
 
 
 def hand_over(low, anc, low_out, anc_out, sem):
@@ -681,6 +736,7 @@
     pieces, raw = anc_row, anc_row // 2
     chips = rows // 2
     places = 1 + pl.cdiv(rows - 2, chips)
+    slots_z = 4 if layers == 4 else layers + 1
     assert levels == 2 and layers == rows and layers % 2 == 0 and layers > 3 and cols <= rows
     assert cols * narrow == share and anc_row % 2 == 0
     any_space = pl.BlockSpec(memory_space=pltpu.HBM)
@@ -706,26 +762,23 @@
             pltpu.VMEM((places, cols, share, width), BF16),
             pltpu.VMEM((cases, width), F32),
             pltpu.VMEM((cases, anc_row * width), F32),
-            pltpu.VMEM((cols, rows, pieces, narrow, width), BF16),
+            pltpu.VMEM((cols * rows * pieces, narrow, width), BF16),
             pltpu.VMEM((cols - 1, rows, pieces, narrow, width), BF16),
             pltpu.VMEM((rows - 1, pieces, narrow, width), BF16),
-            pltpu.VMEM((layers + 1, pieces, narrow, width), BF16),
+            pltpu.VMEM((slots_z, pieces, narrow, width), BF16),
             pltpu.VMEM((2, cols, raw, narrow, width), BF16),
             pltpu.VMEM((cols, pieces - raw, narrow, width), BF16),
             pltpu.SMEM((levels, slots), jnp.int32),
             dma((9,)),
-            dma((rows, chips)),
+            dma,
             dma((places, cols)),
-            dma((rows, rows - 1)),
+            dma((rows - 1,)),
             dma((rows,)),
-            dma((cols - 1, rows, pieces)),
-            dma((cols - 1, rows, pieces)),
-            dma((rows - 1, pieces)),
-            dma((layers + 1, pieces)),
-            dma((cols, raw)),
-            dma((2, cols, raw)),
-            dma((cols, pieces - raw)),
-            dma((cols, pieces - raw)),
+            dma((cols - 1, rows * pieces - raw)),
+            dma((slots_z, pieces)),
+            dma((2, (cols - 1) * raw + 1)),
+            dma(((cols - 1) * (pieces - raw) + 1,)),
+            dma,
         ],
         compiler_params=pltpu.CompilerParams(
             collective_id=0, has_side_effects=True, vmem_limit_bytes=56 * 1024 * 1024

time: 29.1 us -> 28.1 us (0.966)
  the two profiles are of different devices: /device:TPU:21 before, /device:TPU:0 now
where the time goes in v4:
time: 28.1 us; the launch traced here: 27.8 us
  Pallas kernels  27.2 us (97%)
  between operations  0.64 us (2%)
    pallas_call x1, Pallas kernels, on_device(): pl.pallas_call(functools.partial(kernel, sizes), out_shape=(pltpu.VMEM((l...  26.3 us
    pallas_call x1, Pallas kernels, on_device(): pl.pallas_call(hand_over, out_shape=(jax.ShapeDtypeStruct(low.shape, low....  0.83 us

profile of v4, /device:TPU:0, one launch (start us, length us, event | category | flops | bytes accessed | tf_op | source)
XLA Modules:
  0.0 27.8 jit_solution(9506311855968705069)
XLA Ops:
  0.6 26.3 %shard_map.77 = (bf16[2,384,128]{2,1,0:T(8,128)(2,1)S(1)}, f32[4,64,384]{2,1,0:T(8,128)S(1)}) custom-call(s32[2,4]{1,0:T(2,128)} %bitcast.13, bf16[2,384,512]{2,1,0:T(8,128)(2,1)} %bitcast.10, bf16[2,384,384]{2,1,0:T(8,128)(2,1)} %bitcast.11, bf16[2,4,384,384]{3,2,1,0:T(8,128)(2,1)} %bitcast.9, bf16[4,64,384]{2,1,0:T(8,128)(2,1)} %bitcast.12, ...), custom_call_target="tpu_custom_call" | custom-call | tf_op jit(solution)/shard_map/pallas_call | solution.py:744
  27.0 0.8 %shard_map.78 = (bf16[2,384,128]{2,1,0:T(8,128)(2,1)}, f32[4,64,384]{2,1,0:T(8,128)}) custom-call(bf16[2,384,128]{2,1,0:T(8,128)(2,1)S(1)} %get-tuple-element.6.low, f32[4,64,384]{2,1,0:T(8,128)S(1)} %get-tuple-element.7.anc), custom_call_target="tpu_custom_call" | custom-call | tf_op jit(solution)/shard_map/pallas_call | solution.py:794

commit v5 on v4

--- a/solution.py
+++ b/solution.py
@@ -70,7 +70,6 @@
     z_out,
     z_in,
     r_in,
-    e_in,
     targets,
     load_sem,
     p_send,
@@ -80,7 +79,6 @@
     y_recv,
     z_recv,
     r_recv,
-    e_recv,
     send_sem,
 ):
     layers, rows, cols = sizes
@@ -101,15 +99,18 @@
     owner = (1 + col) % rows
 
     loads = [
-        pltpu.make_async_copy(inv_hbm.at[0], inv.at[0], load_sem.at[0]),
-        pltpu.make_async_copy(rhs_hbm.at[0], rhs.at[0], load_sem.at[1]),
-        pltpu.make_async_copy(blocks_hbm.at[0], blocks0, load_sem.at[2]),
-        pltpu.make_async_copy(inv_hbm.at[1], inv.at[1], load_sem.at[3]),
-        pltpu.make_async_copy(rhs_hbm.at[1], rhs.at[1], load_sem.at[4]),
-        pltpu.make_async_copy(blocks_hbm.at[1], blocks1, load_sem.at[5]),
-        pltpu.make_async_copy(inv_anc_hbm, inv_anc, load_sem.at[6]),
-        pltpu.make_async_copy(rhs_anc_hbm, rhs_anc, load_sem.at[7]),
-        pltpu.make_async_copy(targets_hbm, targets, load_sem.at[8]),
+        pltpu.make_async_copy(source, target, load_sem.at[n])
+        for n, source, target in (
+            (0, inv_hbm.at[0], inv.at[0]),
+            (1, rhs_hbm.at[0], rhs.at[0]),
+            (2, blocks_hbm.at[0], blocks0),
+            (0, inv_hbm.at[1], inv.at[1]),
+            (1, rhs_hbm.at[1], rhs.at[1]),
+            (2, blocks_hbm.at[1], blocks1),
+            (3, inv_anc_hbm, inv_anc),
+            (0, rhs_anc_hbm, rhs_anc),
+            (3, targets_hbm, targets),
+        )
     ]
     for n in (0, 1):
         loads[n].start()
@@ -143,7 +144,7 @@
     met = (rows - 1) + (cols - 1) + flag(layer > 0) + flag(layer < last)
     met = met + (cols - 1) + flag(jnp.logical_and(active, col != goal)) * rows
 
-    for n in (8, 2, 3, 4, 5, 6, 7):
+    for n in (8, 2):
         loads[n].start()
 
     def spare(j):
@@ -175,7 +176,7 @@
 
     def solver(k, source):
         if k < 2:
-            return [2 * ch + k for ch in range(chips)]
+            return [2 * ((source // 2 + 1 + ch) % chips) + k for ch in range(chips)]
         return [2 * ((source // 2 + k - 2) % chips)]
 
     def place(k):
@@ -211,8 +212,13 @@
 
     def lower(k):
         if share % 128 == 0:
-            first = jnp.dot(inv[0], rhs[0, :, span(order[k])], preferred_element_type=F32)
-            x0[span(order[k]), :] = first.T.astype(BF16)
+            first = lax.dot_general(
+                rhs[0, :, span(order[k])],
+                inv[0],
+                (((0,), (1,)), ((), ())),
+                preferred_element_type=F32,
+            )
+            x0[span(order[k]), :] = first.astype(BF16)
         elif k == 0:
             first = jnp.dot(inv[0], rhs[0], preferred_element_type=F32)
             x0[...] = first.T.astype(BF16)
@@ -220,10 +226,14 @@
     with scope("ldx0"):
         loads[0].wait()
         loads[1].wait()
+    for n in (3, 4):
+        loads[n].start()
     with scope("x0"):
         lower(0)
     loads[8].wait()
     loads[2].wait()
+    for n in (5, 6):
+        loads[n].start()
 
     @pl.when(active)
     def _():
@@ -248,6 +258,7 @@
                 lower(k)
 
     loads[3].wait()
+    loads[7].start()
     loads[4].wait()
     rhs_t[...] = rhs[1].astype(F32).T
 
@@ -262,15 +273,20 @@
         def _():
             low_out[0] = x0[j * share : (j + 1) * share, :].astype(F32).T.astype(BF16)
 
-    for edge, one, two in ((0, 0, spare(0)), (last, spare(last), last)):
-
+    def blank(edge, slot, h):
         @pl.when(layer == edge)
         def _():
-            for h in range(pieces):
-                if h < raw:
-                    z_in[one, h] = jnp.zeros_like(z_in[one, h])
-                elif layers == 4:
-                    z_in[two, h] = jnp.zeros_like(z_in[two, h])
+            z_in[slot, h] = jnp.zeros_like(z_in[slot, h])
+
+    for h in range(pieces):
+        if h < raw:
+            blank(0, 0, h)
+        elif layers == 4:
+            blank(0, spare(0), h)
+        if h <= raw:
+            blank(last, spare(last), h)
+        elif layers == 4:
+            blank(last, last, h)
 
     loads[5].wait()
 
@@ -288,7 +304,7 @@
         return pltpu.make_async_remote_copy(
             src_ref=x1.at[order[k]],
             dst_ref=x1.at[order[k]],
-            send_sem=x_send.at[k - 1],
+            send_sem=x_send.at[place(k)],
             recv_sem=x_recv.at[k],
             device_id={"row": (row + d) % rows},
             device_id_type=MESH,
@@ -308,8 +324,8 @@
         pltpu.make_async_remote_copy(
             src_ref=x1.at[0 : rows - 1],
             dst_ref=x1.at[0 : rows - 1],
-            send_sem=x_send.at[k - 1],
-            recv_sem=x_send.at[k - 1],
+            send_sem=x_send.at[place(k)],
+            recv_sem=x_send.at[place(k)],
             device_id={"row": mate},
             device_id_type=MESH,
         ).wait_send()
@@ -353,8 +369,8 @@
         )
 
     others, whole = range(1, cols), range(1, cols + 1)
-    mixed = [(h, h + raw) for h in range(raw)]
-    plain = [(2 * h, 2 * h + 1) for h in range(raw)]
+    plain = [(h, h + 1) for h in range(0, pieces, 2)]
+    mixed = [(h, h + raw) for h in range(pieces - raw)] + [(h,) for h in range(pieces - raw, raw)]
 
     def products(k):
         @pl.when(core != k if k < 2 else row != solver(k, owner)[0])
@@ -377,6 +393,8 @@
     middle = jnp.logical_or(layer == layers // 2 - 1, layer == layers // 2)
     upper = layer == layers // 2
     beside = jnp.logical_or(layer == layers // 2 - 2, layer == layers // 2 + 1)
+    low = layer < layers // 2
+    high = jnp.logical_not(low)
     onward = layer + 2 * flag(order[0] > layer) - 1
 
 
@@ -391,35 +409,51 @@
                     for n in range(raw):
                         r_copy(cols, n).start()
 
-        elif k == rows - 2 and h >= raw:
-
-            @pl.when(middle)
+            if h == raw - 1:
+
+                @pl.when(jnp.logical_and(end, low))
+                def _():
+                    r_copy(cols, raw).start()
+
+        elif k == 0 and h == raw:
+
+            @pl.when(jnp.logical_and(end, low))
             def _():
                 for d in others:
-                    e_copy(d, h).start()
-                if h == pieces - 1:
-                    for n in range(raw, pieces):
+                    r_copy(d, h).start()
+
+            @pl.when(high)
+            def _():
+                exchange(k, h)
+
+        elif k == rows - 2:
+            if h >= raw:
+
+                @pl.when(jnp.logical_and(middle, low) if h == raw else middle)
+                def _():
+                    for d in others:
+                        e_copy(d, h).start()
+
+            if h == pieces - 1:
+
+                @pl.when(middle)
+                def _():
+                    for n in range(raw + 1, pieces):
                         e_copy(cols, n).start()
 
+                @pl.when(jnp.logical_and(middle, low))
+                def _():
+                    e_copy(cols, raw).start()
+
             @pl.when(jnp.logical_not(middle))
             def _():
                 exchange(k, h)
 
-        elif k == rows - 2:
-
-            @pl.when(jnp.logical_not(middle))
+        elif k == rows - 1 and h >= raw:
+
+            @pl.when(jnp.logical_not(jnp.logical_and(end, low) if h == raw else end))
             def _():
                 exchange(k, h)
-
-        elif k == rows - 1:
-
-            if h < raw:
-                exchange(k, h)
-            else:
-
-                @pl.when(jnp.logical_not(end))
-                def _():
-                    exchange(k, h)
 
         else:
             exchange(k, h)
@@ -429,10 +463,7 @@
             y_copy(d, k, h).start()
 
     def r_place(d, h):
-        return (d - 1) * raw + h if d < cols else (cols - 1) * raw
-
-    def e_place(d, h):
-        return (d - 1) * (pieces - raw) + h - raw if d < cols else (cols - 1) * (pieces - raw)
+        return (d - 1) * (raw + 1) + h if d < cols else (cols - 1) * (raw + 1)
 
     def r_copy(d, h):
         cc = (col + d) % cols
@@ -445,50 +476,75 @@
             device_id_type=MESH,
         )
 
-    def r_wait(slot, d, h):
-        own = d == cols
+    def r_wait(slot, d, h, n):
+        where = r_in.at[slot, d - 1, 0:n] if n else r_in.at[slot, d - 1, h]
         pltpu.make_async_remote_copy(
-            src_ref=r_in.at[slot, d - 1] if own else r_in.at[slot, d - 1, h],
-            dst_ref=r_in.at[slot, d - 1] if own else r_in.at[slot, d - 1, h],
+            src_ref=where,
+            dst_ref=where,
             send_sem=send_sem,
             recv_sem=r_recv.at[slot, r_place(d, h)],
             device_id={"layer": onward},
             device_id_type=MESH,
         ).wait_recv()
 
-    def r_add(slot, k, d, h):
-        if d < cols or h == 0:
-            r_wait(slot, d, h)
+    def r_add(slot, k, d, h, place=0):
         cc = (col + d) % cols
-        value = packed[at(cc, k, h)].astype(F32) + r_in[slot, d - 1, h].astype(F32)
+        value = packed[at(cc, k, h)].astype(F32) + r_in[slot, d - 1, h - place].astype(F32)
         packed[at(cc, k, h)] = value.astype(BF16)
+
+    def r_others(slot, k, wider, then):
+        for h in range(raw):
+            for d in others:
+                r_wait(slot, d, h, 0)
+                r_add(slot, k, d, h)
+            then(h)
+
+        @pl.when(wider)
+        def _():
+            for d in others:
+                r_wait(slot, d, raw, 0)
+                r_add(slot, k, d, raw)
+            then(raw)
+
+    def r_own(slot, k, wider, then):
+        for n, case in ((raw, jnp.logical_not(wider)), (raw + 1, wider)):
+
+            @pl.when(case)
+            def _():
+                r_wait(slot, cols, 0, n)
+                for h in range(n):
+                    r_add(slot, k, cols, h)
+                    then(h)
 
     def e_copy(d, h):
         cc = (col + d) % cols
         return pltpu.make_async_remote_copy(
             src_ref=packed.at[at(cc, rows - 2, h)],
-            dst_ref=e_in.at[d - 1, h - raw],
+            dst_ref=r_in.at[0, d - 1, h - raw],
             send_sem=send_sem,
-            recv_sem=e_recv.at[e_place(d, h)],
+            recv_sem=r_recv.at[0, r_place(d, h - raw)],
             device_id={"layer": order[rows - 2]},
             device_id_type=MESH,
         )
 
-    def e_add(d, h):
-        if d < cols:
-            e_copy(d, h).wait_recv()
-        elif h == raw:
-            pltpu.make_async_remote_copy(
-                src_ref=e_in.at[d - 1],
-                dst_ref=e_in.at[d - 1],
-                send_sem=send_sem,
-                recv_sem=e_recv.at[e_place(d, h)],
-                device_id={"layer": onward},
-                device_id_type=MESH,
-            ).wait_recv()
-        cc = (col + d) % cols
-        value = packed[at(cc, rows - 1, h)].astype(F32) + e_in[d - 1, h - raw].astype(F32)
-        packed[at(cc, rows - 1, h)] = value.astype(BF16)
+    def e_own(n):
+        where = r_in.at[0, cols - 1, pieces - raw - n : pieces - raw]
+        pltpu.make_async_remote_copy(
+            src_ref=where,
+            dst_ref=where,
+            send_sem=send_sem,
+            recv_sem=r_recv.at[0, r_place(cols, 0)],
+            device_id={"layer": onward},
+            device_id_type=MESH,
+        ).wait_recv()
+        for h in range(pieces - n, pieces):
+            r_add(0, rows - 1, cols, h, raw)
+
+    def e_others(h):
+        for d in others:
+            r_wait(0, d, h - raw, 0)
+            r_add(0, rows - 1, d, h, raw)
+        exchange(rows - 1, h)
 
     def z_copy(k, h):
         j = order[k]
@@ -535,7 +591,9 @@
         )
         if k == rows - 2:
             passing = jnp.logical_and(passing, jnp.logical_not(middle))
-            if h >= raw:
+            if h == raw:
+                passing = jnp.logical_and(passing, jnp.logical_not(jnp.logical_and(beside, low)))
+            elif h > raw:
                 passing = jnp.logical_and(passing, jnp.logical_not(beside))
 
         with scope("z%d%d" % (k, h)):
@@ -551,15 +609,21 @@
 
         z_copy(k, h).start()
 
-    for k in range(2):
-
+    def solve_own(k):
         @pl.when(core == k)
         def _():
             with scope("x1"):
                 solve(k)
             mate_copy(k).start()
 
-    first = [(0, h) for h in range(raw, pieces)]
+    def first():
+        @pl.when(high)
+        def _():
+            merge(0, raw)
+
+        for h in range(raw + 1, pieces):
+            merge(0, h)
+
     early = [(k, h) for k in range(1, rows - 2) for h in range(pieces)]
     late = [(rows - 2, h) for h in range(pieces)]
 
@@ -567,6 +631,8 @@
         with scope("p%d" % k):
             products(k)
 
+    solve_own(0)
+    solve_own(1)
     step(0)
     with scope("x1_2"):
         solve_all(2)
@@ -578,64 +644,74 @@
     @pl.when(jnp.logical_not(end))
     def _():
         with scope("rf1"):
-            for h in range(raw):
-                for d in others:
-                    r_add(0, 0, d, h)
-                    r_copy(d, h).start()
+            r_others(0, 0, low, lambda h: [r_copy(d, h).start() for d in others])
+
+    beyond = jnp.logical_and(end, chip != owner // 2)
+
+    @pl.when(end)
+    def _():
+        first()
+
+    @pl.when(beyond)
+    def _():
+        for k, h in early[:raw]:
+            merge(k, h)
 
     for k in range(2, rows - 1):
         step(k)
 
-    @pl.when(end)
+    @pl.when(jnp.logical_and(end, jnp.logical_not(beyond)))
     def _():
-        for k, h in first + early[:raw]:
+        for k, h in early[:raw]:
             merge(k, h)
 
     @pl.when(jnp.logical_not(end))
     def _():
         with scope("rf2"):
-            for h in range(raw):
-                r_add(0, 0, cols, h)
-                r_copy(cols, h).start()
+            r_own(0, 0, low, lambda h: r_copy(cols, h).start())
 
     @pl.when(middle)
     def _():
         with scope("rn"):
-            for h in range(raw):
-                for d in others:
-                    r_add(1, rows - 2, d, h)
-                exchange(rows - 2, h)
+            r_others(1, rows - 2, high, lambda h: exchange(rows - 2, h))
 
     step(rows - 1)
     low_out[1] = x1[row].astype(F32).T.astype(BF16)
 
     @pl.when(middle)
     def _():
-        for k, h in first:
+        first()
+
+        @pl.when(upper)
+        def _():
+            for k, h in early:
+                merge(k, h)
+
+        @pl.when(jnp.logical_not(upper))
+        def _():
+            for k, h in early[:raw]:
+                merge(k, h)
+
+        with scope("rw"):
+            r_own(1, rows - 2, high, lambda h: None)
+
+        for k, h in late[:raw]:
             merge(k, h)
 
-        with scope("rw"):
-            for h in range(raw):
-                r_add(1, rows - 2, cols, h)
-
-        near = late[:raw]
-
         @pl.when(upper)
         def _():
-            for k, h in early[:-2] + near + early[-2:]:
-                merge(k, h)
+            merge(rows - 2, raw)
 
         @pl.when(jnp.logical_not(upper))
         def _():
-            for k, h in early[:raw] + near[:1] + early[raw:-1] + near[1:] + early[-1:]:
+            for k, h in early[raw:]:
                 merge(k, h)
 
     @pl.when(jnp.logical_not(middle))
     def _():
         @pl.when(jnp.logical_not(end))
         def _():
-            for k, h in first:
-                merge(k, h)
+            first()
 
         @pl.when(jnp.logical_not(end))
         def _():
@@ -647,36 +723,45 @@
 
         with scope("e"):
 
+            @pl.when(jnp.logical_and(end, low))
+            def _():
+                e_others(raw)
+
             @pl.when(end)
             def _():
-                for h in range(raw, pieces):
-                    for d in others:
-                        e_add(d, h)
-                    exchange(rows - 1, h)
-                for h in range(raw, pieces):
-                    e_add(cols, h)
+                for h in range(raw + 1, pieces):
+                    e_others(h)
 
         for k, h in late[raw:]:
             merge(k, h)
+
+        with scope("ew"):
+
+            @pl.when(jnp.logical_and(end, low))
+            def _():
+                e_own(pieces - raw)
+
+            @pl.when(jnp.logical_and(end, high))
+            def _():
+                e_own(pieces - raw - 1)
 
     loads[6].wait()
     loads[7].wait()
     for h in range(pieces):
         with scope("zown%d" % h):
-            for slot, edge, far in ((layer, 0, last), (spare(layer), last, 0)):
-                if h < raw:
-
-                    @pl.when(layer != edge)
-                    def _():
-                        z_wait(slot, h)
-
-                elif layers == 4:
-
-                    @pl.when(layer != far)
-                    def _():
-                        z_wait(slot, h)
-
-                else:
+            below, above = layer >= 0, layer >= 0
+            if h < raw:
+                below = layer != 0
+            elif layers == 4:
+                above = layer != 0
+            if h <= raw:
+                above = jnp.logical_and(above, layer != last)
+            elif layers == 4:
+                below = jnp.logical_and(below, layer != last)
+            for slot, case in ((layer, below), (spare(layer), above)):
+
+                @pl.when(case)
+                def _():
                     z_wait(slot, h)
 
         with scope("yown%d" % h):
@@ -706,16 +791,18 @@
             def _():
                 x_sent(k)
 
-        far, every = raw * cols, pieces * (cols - 1)
-        kept = (pieces - raw) * (cols - 1) + every * (rows - 2) + (pieces - raw) + pieces * (rows - 3)
-
-        @pl.when(middle)
-        def _():
-            sends(far + kept + raw * (cols - 1) + raw + (pieces - raw) * cols).wait_send()
-
-        @pl.when(jnp.logical_not(middle))
-        def _():
-            sends(far + kept + every + pieces).wait_send()
+        every = pieces * (cols - 1)
+        for side, out, back in ((low, raw + 1, raw), (high, raw, raw + 1)):
+            kept = out * cols + (pieces - out) * cols + every * (rows - 2) + pieces * (rows - 3)
+            near = back * cols + (pieces - back) * cols
+
+            @pl.when(jnp.logical_and(side, middle))
+            def _():
+                sends(kept + near).wait_send()
+
+            @pl.when(jnp.logical_and(side, jnp.logical_not(middle)))
+            def _():
+                sends(kept + every + pieces).wait_send()
 
 
 def hand_over(low, anc, low_out, anc_out, sem):
@@ -766,18 +853,16 @@
             pltpu.VMEM((cols - 1, rows, pieces, narrow, width), BF16),
             pltpu.VMEM((rows - 1, pieces, narrow, width), BF16),
             pltpu.VMEM((slots_z, pieces, narrow, width), BF16),
-            pltpu.VMEM((2, cols, raw, narrow, width), BF16),
-            pltpu.VMEM((cols, pieces - raw, narrow, width), BF16),
+            pltpu.VMEM((2, cols, raw + 1, narrow, width), BF16),
             pltpu.SMEM((levels, slots), jnp.int32),
-            dma((9,)),
+            dma((4,)),
             dma,
             dma((places, cols)),
-            dma((rows - 1,)),
+            dma((places,)),
             dma((rows,)),
             dma((cols - 1, rows * pieces - raw)),
             dma((slots_z, pieces)),
-            dma((2, (cols - 1) * raw + 1)),
-            dma(((cols - 1) * (pieces - raw) + 1,)),
+            dma((2, (cols - 1) * (raw + 1) + 1)),
             dma,
         ],
         compiler_params=pltpu.CompilerParams(

time: 28.1 us -> 27.5 us (0.979)
  Pallas kernels: 27.2 us -> 26.7 us
    pallas_call x1, Pallas kernels: 26.3 us -> 25.9 us  [on_device(): pl.pallas_call(functools.partial(kernel, sizes), out_shape=(pltpu.VMEM((l...]
where the time goes in v5:
time: 27.5 us; the launch traced here: 27.4 us
  Pallas kernels  26.7 us (97%)
  between operations  0.64 us (2%)
    pallas_call x1, Pallas kernels, on_device(): pl.pallas_call(functools.partial(kernel, sizes), out_shape=(pltpu.VMEM((l...  25.9 us
    pallas_call x1, Pallas kernels, on_device(): pl.pallas_call(hand_over, out_shape=(jax.ShapeDtypeStruct(low.shape, low....  0.83 us

profile of v5, /device:TPU:0, one launch (start us, length us, event | category | flops | bytes accessed | tf_op | source)
XLA Modules:
  0.0 27.4 jit_solution(9277096097016326604)
XLA Ops:
  0.6 25.9 %shard_map.77 = (bf16[2,384,128]{2,1,0:T(8,128)(2,1)S(1)}, f32[4,64,384]{2,1,0:T(8,128)S(1)}) custom-call(s32[2,4]{1,0:T(2,128)} %bitcast.13, bf16[2,384,512]{2,1,0:T(8,128)(2,1)} %bitcast.10, bf16[2,384,384]{2,1,0:T(8,128)(2,1)} %bitcast.11, bf16[2,4,384,384]{3,2,1,0:T(8,128)(2,1)} %bitcast.9, bf16[4,64,384]{2,1,0:T(8,128)(2,1)} %bitcast.12, ...), custom_call_target="tpu_custom_call" | custom-call | tf_op jit(solution)/shard_map/pallas_call | solution.py:831
  26.5 0.8 %shard_map.78 = (bf16[2,384,128]{2,1,0:T(8,128)(2,1)}, f32[4,64,384]{2,1,0:T(8,128)}) custom-call(bf16[2,384,128]{2,1,0:T(8,128)(2,1)S(1)} %get-tuple-element.6.low, f32[4,64,384]{2,1,0:T(8,128)S(1)} %get-tuple-element.7.anc), custom_call_target="tpu_custom_call" | custom-call | tf_op jit(solution)/shard_map/pallas_call | solution.py:879

commit v6 on v5

--- a/solution.py
+++ b/solution.py
@@ -93,7 +93,6 @@
 
     chip, core = row // 2, row % 2
     mate = row + 1 - 2 * core
-    order = ranked(layer, layers)
     goal = (row + rows - 1) % rows
     active = goal < cols
     owner = (1 + col) % rows
@@ -147,6 +146,8 @@
     for n in (8, 2):
         loads[n].start()
 
+    order = ranked(layer, layers)
+
     def spare(j):
         return (1 - j % 2) * last if layers == 4 else layers
 
@@ -682,15 +683,8 @@
     def _():
         first()
 
-        @pl.when(upper)
-        def _():
-            for k, h in early:
-                merge(k, h)
-
-        @pl.when(jnp.logical_not(upper))
-        def _():
-            for k, h in early[:raw]:
-                merge(k, h)
+        for k, h in early[:raw]:
+            merge(k, h)
 
         with scope("rw"):
             r_own(1, rows - 2, high, lambda h: None)
@@ -702,10 +696,8 @@
         def _():
             merge(rows - 2, raw)
 
-        @pl.when(jnp.logical_not(upper))
-        def _():
-            for k, h in early[raw:]:
-                merge(k, h)
+        for k, h in early[raw:]:
+            merge(k, h)
 
     @pl.when(jnp.logical_not(middle))
     def _():

time: 27.5 us -> 27.4 us (level)
  no operation moved by 1% of the time
where the time goes in v6:
time: 27.4 us; the launch traced here: 27.3 us
  Pallas kernels  26.7 us (97%)
  between operations  0.64 us (2%)
    pallas_call x1, Pallas kernels, on_device(): pl.pallas_call(functools.partial(kernel, sizes), out_shape=(pltpu.VMEM((l...  25.8 us
    pallas_call x1, Pallas kernels, on_device(): pl.pallas_call(hand_over, out_shape=(jax.ShapeDtypeStruct(low.shape, low....  0.83 us

profile of v6, /device:TPU:0, one launch (start us, length us, event | category | flops | bytes accessed | tf_op | source)
XLA Modules:
  0.0 27.3 jit_solution(1633680164707314665)
XLA Ops:
  0.6 25.8 %shard_map.77 = (bf16[2,384,128]{2,1,0:T(8,128)(2,1)S(1)}, f32[4,64,384]{2,1,0:T(8,128)S(1)}) custom-call(s32[2,4]{1,0:T(2,128)} %bitcast.13, bf16[2,384,512]{2,1,0:T(8,128)(2,1)} %bitcast.10, bf16[2,384,384]{2,1,0:T(8,128)(2,1)} %bitcast.11, bf16[2,4,384,384]{3,2,1,0:T(8,128)(2,1)} %bitcast.9, bf16[4,64,384]{2,1,0:T(8,128)(2,1)} %bitcast.12, ...), custom_call_target="tpu_custom_call" | custom-call | tf_op jit(solution)/shard_map/pallas_call | solution.py:823
  26.5 0.8 %shard_map.78 = (bf16[2,384,128]{2,1,0:T(8,128)(2,1)}, f32[4,64,384]{2,1,0:T(8,128)}) custom-call(bf16[2,384,128]{2,1,0:T(8,128)(2,1)S(1)} %get-tuple-element.6.low, f32[4,64,384]{2,1,0:T(8,128)S(1)} %get-tuple-element.7.anc), custom_call_target="tpu_custom_call" | custom-call | tf_op jit(solution)/shard_map/pallas_call | solution.py:871

commit v7 on v6

--- a/solution.py
+++ b/solution.py
@@ -634,10 +634,23 @@
 
     solve_own(0)
     solve_own(1)
+    far_chip = chip != owner // 2
+    swapped = jnp.logical_and(layer == 0, core == 1)
+    swap = jnp.logical_and(swapped, far_chip)
+    lag = jnp.logical_and(swapped, jnp.logical_not(far_chip))
+
+    @pl.when(swap)
+    def _():
+        step(1)
+
     step(0)
     with scope("x1_2"):
         solve_all(2)
-    step(1)
+
+    @pl.when(jnp.logical_not(swap))
+    def _():
+        step(1)
+
     with scope("x1_3"):
         for k in range(3, rows):
             solve_all(k)
@@ -647,13 +660,13 @@
         with scope("rf1"):
             r_others(0, 0, low, lambda h: [r_copy(d, h).start() for d in others])
 
-    beyond = jnp.logical_and(end, chip != owner // 2)
-
-    @pl.when(end)
+    ahead = jnp.logical_or(jnp.logical_and(end, far_chip), lag)
+
+    @pl.when(jnp.logical_and(end, jnp.logical_not(lag)))
     def _():
         first()
 
-    @pl.when(beyond)
+    @pl.when(ahead)
     def _():
         for k, h in early[:raw]:
             merge(k, h)
@@ -661,7 +674,7 @@
     for k in range(2, rows - 1):
         step(k)
 
-    @pl.when(jnp.logical_and(end, jnp.logical_not(beyond)))
+    @pl.when(jnp.logical_and(end, jnp.logical_not(ahead)))
     def _():
         for k, h in early[:raw]:
             merge(k, h)
@@ -710,7 +723,14 @@
             for k, h in early[:raw]:
                 merge(k, h)
 
-        for k, h in early[raw:] + late[:raw]:
+        for k, h in early[raw : raw + 1]:
+            merge(k, h)
+
+        @pl.when(lag)
+        def _():
+            first()
+
+        for k, h in early[raw + 1 :] + late[:raw]:
             merge(k, h)
 
         with scope("e"):

time: 27.4 us -> 27.5 us (level)
  no operation moved by 1% of the time
where the time goes in v7:
time: 27.5 us; the launch traced here: 27.3 us
  Pallas kernels  26.6 us (97%)
  between operations  0.64 us (2%)
    pallas_call x1, Pallas kernels, on_device(): pl.pallas_call(functools.partial(kernel, sizes), out_shape=(pltpu.VMEM((l...  25.8 us
    pallas_call x1, Pallas kernels, on_device(): pl.pallas_call(hand_over, out_shape=(jax.ShapeDtypeStruct(low.shape, low....  0.83 us

profile of v7, /device:TPU:0, one launch (start us, length us, event | category | flops | bytes accessed | tf_op | source)
XLA Modules:
  0.0 27.3 jit_solution(339217732038466499)
XLA Ops:
  0.6 25.8 %shard_map.77 = (bf16[2,384,128]{2,1,0:T(8,128)(2,1)S(1)}, f32[4,64,384]{2,1,0:T(8,128)S(1)}) custom-call(s32[2,4]{1,0:T(2,128)} %bitcast.13, bf16[2,384,512]{2,1,0:T(8,128)(2,1)} %bitcast.10, bf16[2,384,384]{2,1,0:T(8,128)(2,1)} %bitcast.11, bf16[2,4,384,384]{3,2,1,0:T(8,128)(2,1)} %bitcast.9, bf16[4,64,384]{2,1,0:T(8,128)(2,1)} %bitcast.12, ...), custom_call_target="tpu_custom_call" | custom-call | tf_op jit(solution)/shard_map/pallas_call | solution.py:843
  26.5 0.8 %shard_map.78 = (bf16[2,384,128]{2,1,0:T(8,128)(2,1)}, f32[4,64,384]{2,1,0:T(8,128)}) custom-call(bf16[2,384,128]{2,1,0:T(8,128)(2,1)S(1)} %get-tuple-element.6.low, f32[4,64,384]{2,1,0:T(8,128)S(1)} %get-tuple-element.7.anc), custom_call_target="tpu_custom_call" | custom-call | tf_op jit(solution)/shard_map/pallas_call | solution.py:891
